TPU v7x, 32 devices: a whole 2x2x4 slice. The times are simulated.
32 devices in a mesh: gx: 8 (over z, x), af: 4 (over y, core).
Axes of the slice: x: 2, y: 2, z: 4, core: 2. Of those that a mesh axis runs over, the one named last changes fastest.
Arguments:
- forcing: float32 [16, 2, 32, 5, 4, 256], P('af', None, 'gx'), may hold values from -6 to 6
- flow: float32 [32, 4, 256], P('gx'), may hold values from 0.2 to 1
- sponge: float32 [32, 4, 256], P('gx'), may hold values from 0.05 to 0.5
- coupling: float32 [5, 5], replicated, may hold values from -1.5 to 1.5
- omega: float32 [2], replicated, may hold values from 1 to 1.6
Outputs:
- basis: float32 [16, 2, 32, 5, 4, 256], P('af', None, 'gx')
- coeff: float32 [16, 16], replicated
All inputs are finite; a program needn't handle non-finite values.
Results may differ from a plain program's by a relative error of at most 0.0001.
Values sent between devices are 32-bit elements; how exact they have to be, the bound alone decides.
No kernel may reach another device: no remote copies, remote signals or barrier semaphores. Data moves between devices by JAX's collectives and lax.ppermute only.
A program may use at most 64 MiB of HBM per device.

v0:
```python
import jax
import jax.numpy as jnp
from jax import lax
from jax.sharding import PartitionSpec as P

FORCINGS = 8
SWEEPS = 8


viscosity = 0.25


def padded_2(array, sides, width):
    for axis, dim in sides:
        size, length = (lax.axis_size(axis), array.shape[dim])
        up = [(i, (i + 1) % size) for i in range(size - 1)]
        down = [(j, i) for i, j in up]
        last = lax.slice_in_dim(array, length - width, length, axis=dim)
        leading = lax.slice_in_dim(array, 0, width, axis=dim)
        before = lax.ppermute(last, axis, up)
        after = lax.ppermute(leading, axis, down)
        array = jnp.concatenate([before, array, after], axis=dim)
    return array


def apply_adjoint(padded, freq, flow, sponge, coupling):
    field = padded[:, :, 1:-1]
    upper = padded[:, :, 2:]
    lower = padded[:, :, :-2]
    radial = jnp.pad(field, ((0, 0), (0, 0), (0, 0), (0, 0), (1, 1), (0, 0)))
    lap = upper + lower + radial[:, :, :, :, 2:, :] + radial[:, :, :, :, :-2, :]
    lap = lap + jnp.roll(field, 1, -1) + jnp.roll(field, -1, -1) - 6.0 * field
    advect = 0.5 * flow[None, None, :, None] * (lower - upper)
    mixed = jnp.einsum("wv,kpxwrt->kpxvrt", coupling, field, precision=lax.Precision.HIGHEST)
    rotate = jnp.stack([freq * field[:, 1], -freq * field[:, 0]], axis=1)
    return sponge[None, None, :, None] * field + rotate - mixed + advect - viscosity * lap


def precondition(resid, freq, sponge, coupling):
    diag_re = sponge[:, None] + 6.0 * viscosity - jnp.diagonal(coupling)[None, :, None, None]
    diag_re = diag_re[None]
    denom = diag_re * diag_re + freq * freq
    p_re = diag_re / denom
    p_im = freq / denom
    part_re = p_re * resid[:, 0] - p_im * resid[:, 1]
    part_im = p_re * resid[:, 1] + p_im * resid[:, 0]
    return jnp.stack([part_re, part_im], axis=1)


def with_faces(field):
    return padded_2(field, (("gx", 2),), 1)


def on_device(forcing, flow, sponge, coupling, omega):
    local_cols = forcing.shape[0]
    column_ids = lax.axis_index("af") * local_cols + jnp.arange(local_cols)
    freq_vec = jnp.where(column_ids < FORCINGS, omega[0], omega[1])
    freq_b = freq_vec[:, None, None, None, None]
    field = precondition(forcing, freq_b, sponge, coupling)
    for sweep in range(SWEEPS):
        padded = with_faces(field)
        image = apply_adjoint(padded, freq_b, flow, sponge, coupling)
        field = field + precondition(forcing - image, freq_b, sponge, coupling)
    all_cols = local_cols * lax.axis_size("af")
    eye_matrix = jnp.eye(all_cols, dtype=jnp.float32)
    regrouped = lax.all_to_all(field, "af", split_axis=4, concat_axis=0, tiled=True)
    flat = regrouped.reshape(all_cols, -1)
    total = flat.shape[1] * lax.axis_size("gx") * lax.axis_size("af")
    local_gram = jnp.dot(flat, flat.T, precision=lax.Precision.HIGHEST)
    partial_gram = lax.psum(local_gram, "af")
    gram = lax.psum(partial_gram, "gx")
    lower_factor = jnp.linalg.cholesky(gram)
    inverse = jax.scipy.linalg.solve_triangular(lower_factor, eye_matrix, lower=True)
    scaled = jnp.dot(inverse, flat, precision=lax.Precision.HIGHEST) * jnp.sqrt(jnp.float32(total))
    basis = lax.all_to_all(
        scaled.reshape(regrouped.shape), "af", split_axis=0, concat_axis=4, tiled=True
    )
    coeff = lower_factor.T / jnp.sqrt(jnp.float32(total))
    return (basis, coeff)


def solution(mesh):
    placed = (
        P("af", None, "gx", None, None, None),
        P("gx", None, None),
        P("gx", None, None),
        P(),
        P(),
    )
    return jax.shard_map(
        on_device,
        mesh=mesh,
        in_specs=placed,
        out_specs=(P("af", None, "gx", None, None, None), P()),
        check_vma=False,
    )
```

profile of v0, /device:TPU:0, one launch (start us, length us, event | category | flops | bytes accessed | tf_op | source)
XLA Modules:
  0.0 230.4 jit_solution(16400706654534699275)
XLA Ops:
  7.8 5.5 %collective-permute-start = (f32[4,2,1,5,4,256]{5,3,4,2,1,0:T(8,128)S(1)}, f32[4,2,1,5,4,256]{5,3,4,2,1,0:T(8,128)S(1)}, u32[]{:S(2)}, u32[]{:S(2)}) collective-permute-start(f32[4,2,1,5,4,256]{5,3,4,2,1,0:T(8,128)S(1)} %get-tuple-element.89), channel_id=1, source_target_pairs={{0,4},{4,8},{8,12},{12,16},{16,20},{20,24},{24,28},{1,5},{5,9},{9,... | collective-permute-start | bytes 491528 | tf_op jit(solution)/shard_map/ppermute | solution.py:20
  17.6 5.8 %collective-permute-done = f32[4,2,1,5,4,256]{5,3,4,2,1,0:T(8,128)S(1)} collective-permute-done((f32[4,2,1,5,4,256]{5,3,4,2,1,0:T(8,128)S(1)}, f32[4,2,1,5,4,256]{5,3,4,2,1,0:T(8,128)S(1)}, u32[]{:S(2)}, u32[]{:S(2)}) %collective-permute-start) | collective-permute-done | bytes 163872 | tf_op jit(solution)/shard_map/ppermute | solution.py:20
  27.9 5.0 %collective-permute-start.2 = (f32[4,2,1,5,4,256]{5,3,4,2,1,0:T(8,128)S(1)}, f32[4,2,1,5,4,256]{5,3,4,2,1,0:T(8,128)S(1)}, u32[]{:S(2)}, u32[]{:S(2)}) collective-permute-start(f32[4,2,1,5,4,256]{5,3,4,2,1,0:T(8,128)S(1)} %get-tuple-element.83), channel_id=1, source_target_pairs={{0,4},{4,8},{8,12},{12,16},{16,20},{20,24},{24,28},{1,5},{5,9},{9,... | collective-permute-start | bytes 491528 | tf_op jit(solution)/shard_map/ppermute | solution.py:20
  37.5 5.8 %collective-permute-done.2 = f32[4,2,1,5,4,256]{5,3,4,2,1,0:T(8,128)S(1)} collective-permute-done((f32[4,2,1,5,4,256]{5,3,4,2,1,0:T(8,128)S(1)}, f32[4,2,1,5,4,256]{5,3,4,2,1,0:T(8,128)S(1)}, u32[]{:S(2)}, u32[]{:S(2)}) %collective-permute-start.2) | collective-permute-done | bytes 163872 | tf_op jit(solution)/shard_map/ppermute | solution.py:20
  47.9 5.0 %collective-permute-start.4 = (f32[4,2,1,5,4,256]{5,3,4,2,1,0:T(8,128)S(1)}, f32[4,2,1,5,4,256]{5,3,4,2,1,0:T(8,128)S(1)}, u32[]{:S(2)}, u32[]{:S(2)}) collective-permute-start(f32[4,2,1,5,4,256]{5,3,4,2,1,0:T(8,128)S(1)} %get-tuple-element.75), channel_id=1, source_target_pairs={{0,4},{4,8},{8,12},{12,16},{16,20},{20,24},{24,28},{1,5},{5,9},{9,... | collective-permute-start | bytes 491528 | tf_op jit(solution)/shard_map/ppermute | solution.py:20
  53.1 4.3 %collective-permute-done.5 = f32[4,2,1,5,4,256]{5,3,4,2,1,0:T(8,128)S(1)} collective-permute-done((f32[4,2,1,5,4,256]{5,3,4,2,1,0:T(8,128)S(1)}, f32[4,2,1,5,4,256]{5,3,4,2,1,0:T(8,128)S(1)}, u32[]{:S(2)}, u32[]{:S(2)}) %collective-permute-start.5) | collective-permute-done | bytes 163872 | tf_op jit(solution)/shard_map/ppermute | solution.py:21
  57.5 5.8 %collective-permute-done.4 = f32[4,2,1,5,4,256]{5,3,4,2,1,0:T(8,128)S(1)} collective-permute-done((f32[4,2,1,5,4,256]{5,3,4,2,1,0:T(8,128)S(1)}, f32[4,2,1,5,4,256]{5,3,4,2,1,0:T(8,128)S(1)}, u32[]{:S(2)}, u32[]{:S(2)}) %collective-permute-start.4) | collective-permute-done | bytes 163872 | tf_op jit(solution)/shard_map/ppermute | solution.py:20
  68.0 5.2 %collective-permute-start.6 = (f32[4,2,1,5,4,256]{5,3,4,2,1,0:T(8,128)S(1)}, f32[4,2,1,5,4,256]{5,3,4,2,1,0:T(8,128)S(1)}, u32[]{:S(2)}, u32[]{:S(2)}) collective-permute-start(f32[4,2,1,5,4,256]{5,3,4,2,1,0:T(8,128)S(1)} %get-tuple-element.67), channel_id=1, source_target_pairs={{0,4},{4,8},{8,12},{12,16},{16,20},{20,24},{24,28},{1,5},{5,9},{9,... | collective-permute-start | bytes 491528 | tf_op jit(solution)/shard_map/ppermute | solution.py:20
  77.6 5.8 %collective-permute-done.6 = f32[4,2,1,5,4,256]{5,3,4,2,1,0:T(8,128)S(1)} collective-permute-done((f32[4,2,1,5,4,256]{5,3,4,2,1,0:T(8,128)S(1)}, f32[4,2,1,5,4,256]{5,3,4,2,1,0:T(8,128)S(1)}, u32[]{:S(2)}, u32[]{:S(2)}) %collective-permute-start.6) | collective-permute-done | bytes 163872 | tf_op jit(solution)/shard_map/ppermute | solution.py:20
  88.2 5.0 %collective-permute-start.8 = (f32[4,2,1,5,4,256]{5,3,4,2,1,0:T(8,128)S(1)}, f32[4,2,1,5,4,256]{5,3,4,2,1,0:T(8,128)S(1)}, u32[]{:S(2)}, u32[]{:S(2)}) collective-permute-start(f32[4,2,1,5,4,256]{5,3,4,2,1,0:T(8,128)S(1)} %get-tuple-element.59), channel_id=1, source_target_pairs={{0,4},{4,8},{8,12},{12,16},{16,20},{20,24},{24,28},{1,5},{5,9},{9,... | collective-permute-start | bytes 491528 | tf_op jit(solution)/shard_map/ppermute | solution.py:20
  93.5 4.3 %collective-permute-done.9 = f32[4,2,1,5,4,256]{5,3,4,2,1,0:T(8,128)S(1)} collective-permute-done((f32[4,2,1,5,4,256]{5,3,4,2,1,0:T(8,128)S(1)}, f32[4,2,1,5,4,256]{5,3,4,2,1,0:T(8,128)S(1)}, u32[]{:S(2)}, u32[]{:S(2)}) %collective-permute-start.9) | collective-permute-done | bytes 163872 | tf_op jit(solution)/shard_map/ppermute | solution.py:21
  97.8 5.8 %collective-permute-done.8 = f32[4,2,1,5,4,256]{5,3,4,2,1,0:T(8,128)S(1)} collective-permute-done((f32[4,2,1,5,4,256]{5,3,4,2,1,0:T(8,128)S(1)}, f32[4,2,1,5,4,256]{5,3,4,2,1,0:T(8,128)S(1)}, u32[]{:S(2)}, u32[]{:S(2)}) %collective-permute-start.8) | collective-permute-done | bytes 163872 | tf_op jit(solution)/shard_map/ppermute | solution.py:20
  108.6 5.0 %collective-permute-start.10 = (f32[4,2,1,5,4,256]{5,3,4,2,1,0:T(8,128)S(1)}, f32[4,2,1,5,4,256]{5,3,4,2,1,0:T(8,128)S(1)}, u32[]{:S(2)}, u32[]{:S(2)}) collective-permute-start(f32[4,2,1,5,4,256]{5,3,4,2,1,0:T(8,128)S(1)} %get-tuple-element.51), channel_id=1, source_target_pairs={{0,4},{4,8},{8,12},{12,16},{16,20},{20,24},{24,28},{1,5},{5,9},{9,... | collective-permute-start | bytes 491528 | tf_op jit(solution)/shard_map/ppermute | solution.py:20
  113.8 4.3 %collective-permute-done.11 = f32[4,2,1,5,4,256]{5,3,4,2,1,0:T(8,128)S(1)} collective-permute-done((f32[4,2,1,5,4,256]{5,3,4,2,1,0:T(8,128)S(1)}, f32[4,2,1,5,4,256]{5,3,4,2,1,0:T(8,128)S(1)}, u32[]{:S(2)}, u32[]{:S(2)}) %collective-permute-start.11) | collective-permute-done | bytes 163872 | tf_op jit(solution)/shard_map/ppermute | solution.py:21
  118.1 5.8 %collective-permute-done.10 = f32[4,2,1,5,4,256]{5,3,4,2,1,0:T(8,128)S(1)} collective-permute-done((f32[4,2,1,5,4,256]{5,3,4,2,1,0:T(8,128)S(1)}, f32[4,2,1,5,4,256]{5,3,4,2,1,0:T(8,128)S(1)}, u32[]{:S(2)}, u32[]{:S(2)}) %collective-permute-start.10) | collective-permute-done | bytes 163872 | tf_op jit(solution)/shard_map/ppermute | solution.py:20
  129.0 5.2 %collective-permute-start.12 = (f32[4,2,1,5,4,256]{5,3,4,2,1,0:T(8,128)S(1)}, f32[4,2,1,5,4,256]{5,3,4,2,1,0:T(8,128)S(1)}, u32[]{:S(2)}, u32[]{:S(2)}) collective-permute-start(f32[4,2,1,5,4,256]{5,3,4,2,1,0:T(8,128)S(1)} %get-tuple-element.43), channel_id=1, source_target_pairs={{0,4},{4,8},{8,12},{12,16},{16,20},{20,24},{24,28},{1,5},{5,9},{9,... | collective-permute-start | bytes 491528 | tf_op jit(solution)/shard_map/ppermute | solution.py:20
  138.6 5.8 %collective-permute-done.12 = f32[4,2,1,5,4,256]{5,3,4,2,1,0:T(8,128)S(1)} collective-permute-done((f32[4,2,1,5,4,256]{5,3,4,2,1,0:T(8,128)S(1)}, f32[4,2,1,5,4,256]{5,3,4,2,1,0:T(8,128)S(1)}, u32[]{:S(2)}, u32[]{:S(2)}) %collective-permute-start.12) | collective-permute-done | bytes 163872 | tf_op jit(solution)/shard_map/ppermute | solution.py:20
  149.5 5.0 %collective-permute-start.14 = (f32[4,2,1,5,4,256]{5,3,4,2,1,0:T(8,128)S(1)}, f32[4,2,1,5,4,256]{5,3,4,2,1,0:T(8,128)S(1)}, u32[]{:S(2)}, u32[]{:S(2)}) collective-permute-start(f32[4,2,1,5,4,256]{5,3,4,2,1,0:T(8,128)S(1)} %get-tuple-element.35), channel_id=1, source_target_pairs={{0,4},{4,8},{8,12},{12,16},{16,20},{20,24},{24,28},{1,5},{5,9},{9,... | collective-permute-start | bytes 491528 | tf_op jit(solution)/shard_map/ppermute | solution.py:20
  154.8 4.3 %collective-permute-done.15 = f32[4,2,1,5,4,256]{5,3,4,2,1,0:T(8,128)S(1)} collective-permute-done((f32[4,2,1,5,4,256]{5,3,4,2,1,0:T(8,128)S(1)}, f32[4,2,1,5,4,256]{5,3,4,2,1,0:T(8,128)S(1)}, u32[]{:S(2)}, u32[]{:S(2)}) %collective-permute-start.15) | collective-permute-done | bytes 163872 | tf_op jit(solution)/shard_map/ppermute | solution.py:21
  159.1 5.8 %collective-permute-done.14 = f32[4,2,1,5,4,256]{5,3,4,2,1,0:T(8,128)S(1)} collective-permute-done((f32[4,2,1,5,4,256]{5,3,4,2,1,0:T(8,128)S(1)}, f32[4,2,1,5,4,256]{5,3,4,2,1,0:T(8,128)S(1)}, u32[]{:S(2)}, u32[]{:S(2)}) %collective-permute-start.14) | collective-permute-done | bytes 163872 | tf_op jit(solution)/shard_map/ppermute | solution.py:20
  168.9 12.8 %all_to_all.33 = f32[4,2,4,5,4,256]{5,2,3,1,0,4:T(4,128)S(1)} all-to-all(f32[4,2,4,5,4,256]{5,2,3,1,0,4:T(4,128)S(1)} %copy.46), channel_id=1, replica_groups=mesh['gx'=8,'af'=4] {'af'}, dimensions={4} | all-to-all | bytes 1310720 | tf_op jit(solution)/shard_map/all_to_all | solution.py:66
  183.1 5.9 %psum.14 = f32[16,16]{0,1:T(8,128)S(1)} all-reduce(f32[16,16]{0,1:T(8,128)S(1)} %fusion.105), channel_id=1, replica_groups=mesh['gx'=8,'af'=4] {'af'}, use_global_device_ids=true, to_apply=%region_0.1 | all-reduce | flops 256 | bytes 2048 | tf_op jit(solution)/shard_map/psum | solution.py:70
  189.0 20.1 %psum.15 = f32[16,16]{0,1:T(8,128)S(1)} all-reduce(f32[16,16]{0,1:T(8,128)S(1)} %psum.14), channel_id=1, replica_groups=mesh['gx'=8,'af'=4] {'gx'}, use_global_device_ids=true, to_apply=%region_1.2 | all-reduce | flops 256 | bytes 2048 | tf_op jit(solution)/shard_map/psum | solution.py:71
  219.7 9.5 %all-to-all-done.1 = f32[16,2,4,5,1,256]{5,2,4,3,1,0:T(4,128)S(1)} async-done(((f32[16,2,4,5,1,256]{5,2,4,3,1,0:T(4,128)}), f32[16,2,4,5,1,256]{5,2,4,3,1,0:T(4,128)S(1)}, u32[]{:S(2)}, u32[]{:S(2)}) %all-to-all-start.1) | async-done | bytes 655392 | tf_op jit(solution)/shard_map/all_to_all | solution.py:75
  (104 shorter events, 76.3 us)
Async XLA Ops:
  0.6 4.7 %copy-start = (f32[5,5]{1,0:T(8,128)S(1)}, f32[5,5]{1,0:T(8,128)}, u32[]{:S(2)}) copy-start(f32[5,5]{1,0:T(8,128)} %param.8) | copy-start | bytes 304
  6.5 11.2 %collective-permute-start.1 = (f32[4,2,1,5,4,256]{5,3,4,2,1,0:T(8,128)S(1)}, f32[4,2,1,5,4,256]{5,3,4,2,1,0:T(8,128)S(1)}, u32[]{:S(2)}, u32[]{:S(2)}) collective-permute-start(f32[4,2,1,5,4,256]{5,3,4,2,1,0:T(8,128)S(1)} %get-tuple-element.88), channel_id=1, source_target_pairs={{4,0},{8,4},{12,8},{16,12},{20,16},{24,20},{28,24},{5,1},{9,5},{13... | collective-permute-start | bytes 491528 | tf_op jit(solution)/shard_map/ppermute | solution.py:21
  7.8 15.6 %collective-permute-start = (f32[4,2,1,5,4,256]{5,3,4,2,1,0:T(8,128)S(1)}, f32[4,2,1,5,4,256]{5,3,4,2,1,0:T(8,128)S(1)}, u32[]{:S(2)}, u32[]{:S(2)}) collective-permute-start(f32[4,2,1,5,4,256]{5,3,4,2,1,0:T(8,128)S(1)} %get-tuple-element.89), channel_id=1, source_target_pairs={{0,4},{4,8},{8,12},{12,16},{16,20},{20,24},{24,28},{1,5},{5,9},{9,... | collective-permute-start | bytes 491528 | tf_op jit(solution)/shard_map/ppermute | solution.py:20
  13.4 0.7 copy-start.2
  14.1 9.3 %copy-start.1 = (f32[4,2,4,5,4,256]{5,4,3,2,1,0:T(4,128)S(1)}, f32[4,2,4,5,4,256]{5,4,3,2,1,0:T(4,128)}, u32[]{:S(2)}) copy-start(f32[4,2,4,5,4,256]{5,4,3,2,1,0:T(4,128)} %param.5) | copy-start | bytes 1966084
  14.1 9.3 %copy-start.3 = (f32[4,4,256]{2,1,0:T(4,128)S(1)}, f32[4,4,256]{2,1,0:T(4,128)}, u32[]{:S(2)}) copy-start(f32[4,4,256]{2,1,0:T(4,128)} %param.7) | copy-start | bytes 49156
  26.6 10.9 %collective-permute-start.3 = (f32[4,2,1,5,4,256]{5,3,4,2,1,0:T(8,128)S(1)}, f32[4,2,1,5,4,256]{5,3,4,2,1,0:T(8,128)S(1)}, u32[]{:S(2)}, u32[]{:S(2)}) collective-permute-start(f32[4,2,1,5,4,256]{5,3,4,2,1,0:T(8,128)S(1)} %get-tuple-element.82), channel_id=1, source_target_pairs={{4,0},{8,4},{12,8},{16,12},{20,16},{24,20},{28,24},{5,1},{9,5},{13... | collective-permute-start | bytes 491528 | tf_op jit(solution)/shard_map/ppermute | solution.py:21
  27.9 15.3 %collective-permute-start.2 = (f32[4,2,1,5,4,256]{5,3,4,2,1,0:T(8,128)S(1)}, f32[4,2,1,5,4,256]{5,3,4,2,1,0:T(8,128)S(1)}, u32[]{:S(2)}, u32[]{:S(2)}) collective-permute-start(f32[4,2,1,5,4,256]{5,3,4,2,1,0:T(8,128)S(1)} %get-tuple-element.83), channel_id=1, source_target_pairs={{0,4},{4,8},{8,12},{12,16},{16,20},{20,24},{24,28},{1,5},{5,9},{9,... | collective-permute-start | bytes 491528 | tf_op jit(solution)/shard_map/ppermute | solution.py:20
  46.6 10.9 %collective-permute-start.5 = (f32[4,2,1,5,4,256]{5,3,4,2,1,0:T(8,128)S(1)}, f32[4,2,1,5,4,256]{5,3,4,2,1,0:T(8,128)S(1)}, u32[]{:S(2)}, u32[]{:S(2)}) collective-permute-start(f32[4,2,1,5,4,256]{5,3,4,2,1,0:T(8,128)S(1)} %get-tuple-element.74), channel_id=1, source_target_pairs={{4,0},{8,4},{12,8},{16,12},{20,16},{24,20},{28,24},{5,1},{9,5},{13... | collective-permute-start | bytes 491528 | tf_op jit(solution)/shard_map/ppermute | solution.py:21
  47.9 15.3 %collective-permute-start.4 = (f32[4,2,1,5,4,256]{5,3,4,2,1,0:T(8,128)S(1)}, f32[4,2,1,5,4,256]{5,3,4,2,1,0:T(8,128)S(1)}, u32[]{:S(2)}, u32[]{:S(2)}) collective-permute-start(f32[4,2,1,5,4,256]{5,3,4,2,1,0:T(8,128)S(1)} %get-tuple-element.75), channel_id=1, source_target_pairs={{0,4},{4,8},{8,12},{12,16},{16,20},{20,24},{24,28},{1,5},{5,9},{9,... | collective-permute-start | bytes 491528 | tf_op jit(solution)/shard_map/ppermute | solution.py:20
  66.7 10.9 %collective-permute-start.7 = (f32[4,2,1,5,4,256]{5,3,4,2,1,0:T(8,128)S(1)}, f32[4,2,1,5,4,256]{5,3,4,2,1,0:T(8,128)S(1)}, u32[]{:S(2)}, u32[]{:S(2)}) collective-permute-start(f32[4,2,1,5,4,256]{5,3,4,2,1,0:T(8,128)S(1)} %get-tuple-element.66), channel_id=1, source_target_pairs={{4,0},{8,4},{12,8},{16,12},{20,16},{24,20},{28,24},{5,1},{9,5},{13... | collective-permute-start | bytes 491528 | tf_op jit(solution)/shard_map/ppermute | solution.py:21
  68.0 15.3 %collective-permute-start.6 = (f32[4,2,1,5,4,256]{5,3,4,2,1,0:T(8,128)S(1)}, f32[4,2,1,5,4,256]{5,3,4,2,1,0:T(8,128)S(1)}, u32[]{:S(2)}, u32[]{:S(2)}) collective-permute-start(f32[4,2,1,5,4,256]{5,3,4,2,1,0:T(8,128)S(1)} %get-tuple-element.67), channel_id=1, source_target_pairs={{0,4},{4,8},{8,12},{12,16},{16,20},{20,24},{24,28},{1,5},{5,9},{9,... | collective-permute-start | bytes 491528 | tf_op jit(solution)/shard_map/ppermute | solution.py:20
  86.9 10.9 %collective-permute-start.9 = (f32[4,2,1,5,4,256]{5,3,4,2,1,0:T(8,128)S(1)}, f32[4,2,1,5,4,256]{5,3,4,2,1,0:T(8,128)S(1)}, u32[]{:S(2)}, u32[]{:S(2)}) collective-permute-start(f32[4,2,1,5,4,256]{5,3,4,2,1,0:T(8,128)S(1)} %get-tuple-element.58), channel_id=1, source_target_pairs={{4,0},{8,4},{12,8},{16,12},{20,16},{24,20},{28,24},{5,1},{9,5},{13... | collective-permute-start | bytes 491528 | tf_op jit(solution)/shard_map/ppermute | solution.py:21
  88.2 15.3 %collective-permute-start.8 = (f32[4,2,1,5,4,256]{5,3,4,2,1,0:T(8,128)S(1)}, f32[4,2,1,5,4,256]{5,3,4,2,1,0:T(8,128)S(1)}, u32[]{:S(2)}, u32[]{:S(2)}) collective-permute-start(f32[4,2,1,5,4,256]{5,3,4,2,1,0:T(8,128)S(1)} %get-tuple-element.59), channel_id=1, source_target_pairs={{0,4},{4,8},{8,12},{12,16},{16,20},{20,24},{24,28},{1,5},{5,9},{9,... | collective-permute-start | bytes 491528 | tf_op jit(solution)/shard_map/ppermute | solution.py:20
  107.3 10.9 %collective-permute-start.11 = (f32[4,2,1,5,4,256]{5,3,4,2,1,0:T(8,128)S(1)}, f32[4,2,1,5,4,256]{5,3,4,2,1,0:T(8,128)S(1)}, u32[]{:S(2)}, u32[]{:S(2)}) collective-permute-start(f32[4,2,1,5,4,256]{5,3,4,2,1,0:T(8,128)S(1)} %get-tuple-element.50), channel_id=1, source_target_pairs={{4,0},{8,4},{12,8},{16,12},{20,16},{24,20},{28,24},{5,1},{9,5},{13... | collective-permute-start | bytes 491528 | tf_op jit(solution)/shard_map/ppermute | solution.py:21
  108.6 15.3 %collective-permute-start.10 = (f32[4,2,1,5,4,256]{5,3,4,2,1,0:T(8,128)S(1)}, f32[4,2,1,5,4,256]{5,3,4,2,1,0:T(8,128)S(1)}, u32[]{:S(2)}, u32[]{:S(2)}) collective-permute-start(f32[4,2,1,5,4,256]{5,3,4,2,1,0:T(8,128)S(1)} %get-tuple-element.51), channel_id=1, source_target_pairs={{0,4},{4,8},{8,12},{12,16},{16,20},{20,24},{24,28},{1,5},{5,9},{9,... | collective-permute-start | bytes 491528 | tf_op jit(solution)/shard_map/ppermute | solution.py:20
  127.7 10.9 %collective-permute-start.13 = (f32[4,2,1,5,4,256]{5,3,4,2,1,0:T(8,128)S(1)}, f32[4,2,1,5,4,256]{5,3,4,2,1,0:T(8,128)S(1)}, u32[]{:S(2)}, u32[]{:S(2)}) collective-permute-start(f32[4,2,1,5,4,256]{5,3,4,2,1,0:T(8,128)S(1)} %get-tuple-element.42), channel_id=1, source_target_pairs={{4,0},{8,4},{12,8},{16,12},{20,16},{24,20},{28,24},{5,1},{9,5},{13... | collective-permute-start | bytes 491528 | tf_op jit(solution)/shard_map/ppermute | solution.py:21
  129.0 15.3 %collective-permute-start.12 = (f32[4,2,1,5,4,256]{5,3,4,2,1,0:T(8,128)S(1)}, f32[4,2,1,5,4,256]{5,3,4,2,1,0:T(8,128)S(1)}, u32[]{:S(2)}, u32[]{:S(2)}) collective-permute-start(f32[4,2,1,5,4,256]{5,3,4,2,1,0:T(8,128)S(1)} %get-tuple-element.43), channel_id=1, source_target_pairs={{0,4},{4,8},{8,12},{12,16},{16,20},{20,24},{24,28},{1,5},{5,9},{9,... | collective-permute-start | bytes 491528 | tf_op jit(solution)/shard_map/ppermute | solution.py:20
  148.2 10.9 %collective-permute-start.15 = (f32[4,2,1,5,4,256]{5,3,4,2,1,0:T(8,128)S(1)}, f32[4,2,1,5,4,256]{5,3,4,2,1,0:T(8,128)S(1)}, u32[]{:S(2)}, u32[]{:S(2)}) collective-permute-start(f32[4,2,1,5,4,256]{5,3,4,2,1,0:T(8,128)S(1)} %get-tuple-element.34), channel_id=1, source_target_pairs={{4,0},{8,4},{12,8},{16,12},{20,16},{24,20},{28,24},{5,1},{9,5},{13... | collective-permute-start | bytes 491528 | tf_op jit(solution)/shard_map/ppermute | solution.py:21
  149.5 15.3 %collective-permute-start.14 = (f32[4,2,1,5,4,256]{5,3,4,2,1,0:T(8,128)S(1)}, f32[4,2,1,5,4,256]{5,3,4,2,1,0:T(8,128)S(1)}, u32[]{:S(2)}, u32[]{:S(2)}) collective-permute-start(f32[4,2,1,5,4,256]{5,3,4,2,1,0:T(8,128)S(1)} %get-tuple-element.35), channel_id=1, source_target_pairs={{0,4},{4,8},{8,12},{12,16},{16,20},{20,24},{24,28},{1,5},{5,9},{9,... | collective-permute-start | bytes 491528 | tf_op jit(solution)/shard_map/ppermute | solution.py:20
  215.5 13.7 %all-to-all-start.1 = ((f32[16,2,4,5,1,256]{5,2,4,3,1,0:T(4,128)}), f32[16,2,4,5,1,256]{5,2,4,3,1,0:T(4,128)S(1)}, u32[]{:S(2)}, u32[]{:S(2)}) async-start(f32[16,2,4,5,1,256]{5,2,4,3,1,0:T(4,128)} %copy.50), calls=%async_computation.1 | async-start | bytes 1310720 | tf_op jit(solution)/shard_map/all_to_all | solution.py:75
where the time goes:
time: 231 us; the launch traced here: 230 us
  waiting for transfers between devices  88.6 us (38%)
  starting transfers between devices  54.9 us (24%)
  blocking collectives  38.7 us (17%)
  matrix products  18.3 us (8%)
  other arithmetic  16 us (7%)
  local copies, waits for them, and re-layouts  12.5 us (5%)
    ppermute x8, waiting for transfers between devices, padded_2(): before = lax.ppermute(last, axis, up)  46.1 us
    ppermute x8, starting transfers between devices, padded_2(): before = lax.ppermute(last, axis, up)  41.1 us
    ppermute x8, waiting for transfers between devices, padded_2(): after = lax.ppermute(leading, axis, down)  33 us
    psum x1, blocking collectives, on_device(): gram = lax.psum(partial_gram, 'gx')  20.1 us
    dot_general x8, matrix products, apply_adjoint(): jnp.einsum('wv,kpxwrt->kpxvrt', coupling, field, precision=lax.Precision....  16.5 us
    all_to_all x1, blocking collectives, on_device(): lax.all_to_all(field, 'af', split_axis=4, concat_axis=0, tiled=True)  12.8 us
    ppermute x8, starting transfers between devices, padded_2(): after = lax.ppermute(leading, axis, down)  10.3 us
    all_to_all x1, waiting for transfers between devices, on_device(): lax.all_to_all(scaled.reshape(regrouped.shape), 'af', split_axis=0, conca...  9.51 us
  transfers between devices with their start and end apart: 17, of which 17 were waited for; matrix products, arithmetic and copies ran while one was open for 1% of the time, Pallas kernels for 0%

commit v1 on v0

v1 whole, which is shorter than its diff:
```python
import functools

import jax
import jax.numpy as jnp
from jax import lax
from jax.experimental import pallas as pl
from jax.experimental.pallas import tpu as pltpu
from jax.sharding import PartitionSpec as P

FORCINGS = 8
SWEEPS = 8

viscosity = 0.25
SUB, LANE = 8, 128
EXACT = lax.Precision.HIGHEST


def fold(plane):
    return jnp.concatenate([plane[:, :LANE], plane[:, LANE:]], axis=0)


def pack_kernel(forcing_ref, sponge_ref, flow_ref, *out_refs):
    cols, parts, planes, nvar = forcing_ref.shape[:4]
    me = lax.rem(lax.axis_index("gx"), cols)
    rows = parts * planes * nvar
    for k, out_ref in enumerate(out_refs):
        col = lax.rem(me + k, cols)
        for part in range(parts):
            for plane in range(planes):
                for v in range(nvar):
                    row = (part * planes + plane) * nvar + v
                    out_ref[row] = fold(forcing_ref[col, part, plane, v])
        for plane in range(planes):
            out_ref[rows + plane] = fold(sponge_ref[plane])
            out_ref[rows + planes + plane] = fold(flow_ref[plane])


def pack(forcing, sponge, flow):
    cols, parts, planes, nvar = forcing.shape[:4]
    rows = planes * (parts * nvar + 2)
    slab = jax.ShapeDtypeStruct((rows, SUB, LANE), jnp.float32)
    return pl.pallas_call(
        pack_kernel,
        out_shape=(slab,) * cols,
        in_specs=[pl.BlockSpec(memory_space=pltpu.VMEM)] * 3,
        out_specs=(pl.BlockSpec(memory_space=pltpu.VMEM),) * cols,
        name="pack",
    )(forcing, sponge, flow)


def locate(i, two_sided, flip, cols, planes, span):
    own = cols * planes
    if two_sided:
        j = i - span
        slab, inner = lax.div(j + span, planes) - span // planes, lax.rem(i, planes)
        slot = jnp.where(slab < 0, slab + 2 * cols, slab)
        return slot, inner, i
    slab, inner = lax.div(i, planes), lax.rem(i, planes)
    far = jnp.where(i < own, cols - 1 - slab, 3 * cols - 1 - slab)
    return jnp.where(flip == 1, far, slab), jnp.where(flip == 1, planes - 1 - inner, inner), i


def sweep_kernel(dims, two_sided, *refs):
    cols, parts, planes, nvar, groups = dims
    coupling_ref, omega_ref = refs[:2]
    slab_refs = refs[2 : 2 + 2 * cols]
    out_ref = refs[2 + 2 * cols]
    raw, first, even, odd, p_re, p_im, w_lo, w_hi, sems = refs[3 + 2 * cols :]
    gx = lax.axis_index("gx")
    me, group = lax.rem(gx, cols), lax.div(gx, cols)
    flip = jnp.int32(0) if two_sided else jnp.int32(group)
    rows = planes * (parts * nvar + 2)
    comp = parts * nvar
    own, span = cols * planes, SWEEPS
    window = own + span * (2 if two_sided else 1)

    copies = []
    for k, slab_ref in enumerate(slab_refs):
        slot = lax.rem(me + cols - k % cols, cols) + cols * (k // cols)
        copies.append(pltpu.make_async_copy(slab_ref, raw.at[pl.ds(slot * rows, rows)], sems.at[k]))
        copies[-1].start()

    column = lax.axis_index("af") * cols + me
    freq = jnp.where(column < FORCINGS, omega_ref[0], omega_ref[1])
    side = jnp.where(flip == 1, -2.0, 2.0).astype(jnp.float32)
    zero = jnp.zeros((SUB, LANE), jnp.float32)
    for ref in (first, even, odd):
        for c in range(comp):
            ref[c] = zero
    for copy in copies:
        copy.wait()

    def prepare(i, _):
        slot, inner, _ = locate(i, two_sided, flip, cols, planes, span)
        base = slot * rows
        sponge = raw[base + planes * comp + inner]
        flow = raw[base + planes * comp + planes + inner]
        w_lo[i] = 1.0 - side * flow
        w_hi[i] = 1.0 + side * flow
        if two_sided:
            inside = jnp.logical_and(
                jnp.logical_or(i >= span, group > 0),
                jnp.logical_or(i < span + own, group < groups - 1),
            )
            keep = jnp.where(inside, 1.0, 0.0).astype(jnp.float32)
        for v in range(nvar):
            diag = sponge + (6.0 * viscosity - coupling_ref[v, v])
            scale = 1.0 / (diag * diag + freq * freq)
            if two_sided:
                scale = scale * keep
            pr, pi = diag * scale, freq * scale
            f_re = raw[base + inner * nvar + v]
            f_im = raw[base + planes * nvar + inner * nvar + v]
            first[(i + 1) * comp + v] = pr * f_re - pi * f_im
            first[(i + 1) * comp + nvar + v] = pr * f_im + pi * f_re
            p_re[i * nvar + v] = viscosity * pr
            p_im[i * nvar + v] = viscosity * pi
        return 0

    lax.fori_loop(0, window, prepare, 0)

    lane = lax.broadcasted_iota(jnp.int32, (SUB, LANE), 1)
    radial = lax.rem(lax.broadcasted_iota(jnp.int32, (SUB, LANE), 0), SUB // 2)
    at_last, at_first = lane == LANE - 1, lane == 0
    at_outer, at_axis = radial == SUB // 2 - 1, radial == 0
    pull = [[coupling_ref[u, v] * (1.0 / viscosity) for v in range(nvar)] for u in range(nvar)]

    def update(i, src, emit):
        field = [src[(i + 1) * comp + c] for c in range(comp)]
        lo, hi = w_lo[i], w_hi[i]
        for v in range(nvar):
            sums = []
            for part in range(parts):
                c = part * nvar + v
                z = field[c]
                other = pltpu.roll(z, SUB // 2, 0)
                total = pltpu.roll(jnp.where(at_last, other, z), 1, 1)
                total = total + pltpu.roll(jnp.where(at_first, other, z), LANE - 1, 1)
                total = total + jnp.where(at_axis, 0.0, pltpu.roll(z, 1, 0))
                total = total + jnp.where(at_outer, 0.0, pltpu.roll(z, SUB - 1, 0))
                total = total + lo * src[i * comp + c]
                total = total + hi * src[(i + 2) * comp + c]
                for u in range(nvar):
                    if u != v:
                        total = total + pull[u][v] * field[part * nvar + u]
                sums.append(total)
            pr, pi = p_re[i * nvar + v], p_im[i * nvar + v]
            emit(i, v, first[(i + 1) * comp + v] + (pr * sums[0] - pi * sums[1]))
            emit(i, nvar + v, first[(i + 1) * comp + nvar + v] + (pr * sums[1] + pi * sums[0]))

    def level(src, emit, lo, hi, unroll):
        def body(n, _):
            for m in range(unroll):
                update(lo + n * unroll + m, src, emit)
            return 0

        trips = (hi - lo) // unroll
        lax.fori_loop(0, trips, body, 0)
        for i in range(lo + trips * unroll, hi):
            update(jnp.int32(i), src, emit)

    def into(ref):
        def emit(i, c, value):
            ref[(i + 1) * comp + c] = value

        return emit

    def finish(i, c, value):
        plane = i - span if two_sided else jnp.where(flip == 1, own - 1 - i, i)
        out_ref[lax.rem(plane, planes) * cols + lax.div(plane, planes), c] = value

    src = first
    for s in range(1, SWEEPS):
        dst = odd if s % 2 else even
        level(src, into(dst), s if two_sided else 0, window - s, 2)
        src = dst
    start = span if two_sided else 0
    level(src, finish, start, start + own, 2)


def sweeps(coupling, omega, slabs, dims, two_sided):
    cols, parts, planes, nvar, groups = dims
    comp = parts * nvar
    rows = planes * (comp + 2)
    own = cols * planes
    window = own + SWEEPS * (2 if two_sided else 1)
    tiles = lambda n: pltpu.VMEM((n, SUB, LANE), jnp.float32)
    return pl.pallas_call(
        functools.partial(sweep_kernel, dims, two_sided),
        out_shape=jax.ShapeDtypeStruct((own, comp, SUB, LANE), jnp.float32),
        in_specs=[pl.BlockSpec(memory_space=pltpu.SMEM)] * 2 + [pl.BlockSpec(memory_space=pl.ANY)] * len(slabs),
        out_specs=pl.BlockSpec(memory_space=pltpu.VMEM),
        scratch_shapes=[
            tiles(2 * cols * rows),
            tiles((window + 2) * comp),
            tiles((window + 2) * comp),
            tiles((window + 2) * comp),
            tiles(window * nvar),
            tiles(window * nvar),
            tiles(window),
            tiles(window),
            pltpu.SemaphoreType.DMA((2 * cols,)),
        ],
        name="sweeps",
    )(coupling, omega, *slabs)


def gram_kernel(y_ref, g_ref):
    count, comp = y_ref.shape[:2]
    rows = count * SUB
    pair = (((1,), (1,)), ((), ()))
    total = jnp.zeros((rows, rows), jnp.float32)
    for c in range(comp):
        part = y_ref[:, c].reshape(rows, LANE)
        total = total + lax.dot_general(part, part, pair, precision=EXACT, preferred_element_type=jnp.float32)
    row = lax.broadcasted_iota(jnp.int32, (rows, rows), 0)
    col = lax.broadcasted_iota(jnp.int32, (rows, rows), 1)
    total = jnp.where(lax.rem(row, SUB) == lax.rem(col, SUB), total, 0.0)
    owner = lax.div(lax.broadcasted_iota(jnp.int32, (count, rows), 1), SUB)
    member = (owner == lax.broadcasted_iota(jnp.int32, (count, rows), 0)).astype(jnp.float32)
    half = lax.dot_general(member, total, (((1,), (0,)), ((), ())), precision=EXACT, preferred_element_type=jnp.float32)
    g_ref[...] = lax.dot_general(half, member, pair, precision=EXACT, preferred_element_type=jnp.float32)


def gram(y):
    return pl.pallas_call(
        gram_kernel,
        out_shape=jax.ShapeDtypeStruct((y.shape[0],) * 2, jnp.float32),
        in_specs=[pl.BlockSpec(memory_space=pltpu.VMEM)],
        out_specs=pl.BlockSpec(memory_space=pltpu.VMEM),
        name="gram",
    )(y)


def factor_kernel(length, g_ref, coeff_ref, linv_ref):
    n = g_ref.shape[0]
    row = lax.broadcasted_iota(jnp.int32, (n, n), 0)
    col = lax.broadcasted_iota(jnp.int32, (n, n), 1)
    left, right = g_ref[...], (row == col).astype(jnp.float32)
    upper, lower = jnp.zeros((n, n), jnp.float32), jnp.zeros((n, n), jnp.float32)
    for k in range(n):
        pivot = left[k : k + 1, k : k + 1]
        left_row, right_row = left[k : k + 1, :], right[k : k + 1, :]
        root = 1.0 / jnp.sqrt(pivot)
        upper = jnp.where(row == k, left_row * root, upper)
        lower = jnp.where(row == k, right_row * root, lower)
        times = jnp.where(row > k, left[:, k : k + 1] / pivot, 0.0)
        left = left - times * left_row
        right = right - times * right_row
    coeff_ref[...] = jnp.where(col >= row, upper, 0.0) / jnp.sqrt(jnp.float32(length))
    linv_ref[...] = lower * jnp.sqrt(jnp.float32(length))


def factor(g, length):
    square = jax.ShapeDtypeStruct(g.shape, jnp.float32)
    return pl.pallas_call(
        functools.partial(factor_kernel, length),
        out_shape=(square, square),
        in_specs=[pl.BlockSpec(memory_space=pltpu.VMEM)],
        out_specs=(pl.BlockSpec(memory_space=pltpu.VMEM),) * 2,
        name="factor",
    )(g)


def basis_kernel(linv_ref, *refs):
    y_refs, out_ref, table = refs[:-2], refs[-2], refs[-1]
    cols, parts, planes, nvar = out_ref.shape[:4]
    count = linv_ref.shape[0]
    af = lax.axis_index("af")
    for c in range(cols):
        line = linv_ref[pl.ds(af * cols + c, 1), :]
        for u in range(count):
            table[c * count + u] = jnp.broadcast_to(line[:, u : u + 1], (SUB, LANE))
    for k, y_ref in enumerate(y_refs):
        plane = lax.bitwise_xor(af, k)
        for part in range(parts):
            sums = [[None] * nvar for _ in range(cols)]
            for u in range(count):
                values = [y_ref[u, part * nvar + v] for v in range(nvar)]
                for c in range(cols):
                    times = table[c * count + u]
                    for v in range(nvar):
                        term = times * values[v]
                        sums[c][v] = term if u == 0 else sums[c][v] + term
            for c in range(cols):
                for v in range(nvar):
                    out_ref[c, part, plane, v, :, :LANE] = sums[c][v][: SUB // 2]
                    out_ref[c, part, plane, v, :, LANE:] = sums[c][v][SUB // 2 :]


def basis_of(linv, ys, shape):
    return pl.pallas_call(
        basis_kernel,
        out_shape=jax.ShapeDtypeStruct(shape, jnp.float32),
        in_specs=[pl.BlockSpec(memory_space=pltpu.VMEM)] * (1 + len(ys)),
        out_specs=pl.BlockSpec(memory_space=pltpu.VMEM),
        scratch_shapes=[pltpu.VMEM((shape[0] * linv.shape[0], SUB, LANE), jnp.float32)],
        name="basis",
    )(linv, *ys)


def on_device(size_x, size_f, forcing, flow, sponge, coupling, omega):
    cols, parts, planes, nvar, rad, azi = forcing.shape
    groups = size_x // cols
    two_sided = groups != 2
    count = cols * size_f
    assert rad * azi == SUB * LANE and azi == 2 * LANE and size_x % cols == 0
    assert planes == size_f and 2 * planes == SWEEPS and cols == 4
    dims = (cols, parts, planes, nvar, groups)

    slabs = pack(forcing, sponge, flow)
    halo = []
    for k in range(cols):
        pairs = []
        for g in range(size_x):
            group, j = divmod(g, cols)
            target = group - 1 if j < cols // 2 else group + 1
            if 0 <= target < groups:
                pairs.append((g, target * cols + (j + k) % cols))
        halo.append(lax.ppermute(slabs[k], "gx", pairs))
    mine = [slabs[0]]
    for k in range(1, cols):
        pairs = [(g, g // cols * cols + (g + k) % cols) for g in range(size_x)]
        mine.append(lax.ppermute(slabs[k], "gx", pairs))
    z = sweeps(coupling, omega, mine + halo, dims, two_sided)

    together = [
        [(q * cols + j) * size_f + a for a in range(size_f) for j in range(cols)] for q in range(groups)
    ]
    y = lax.all_to_all(z, ("gx", "af"), 0, 0, axis_index_groups=together, tiled=True)
    ys = [y] + [None] * (size_f - 1)
    ys[2] = lax.ppermute(y, "af", [(a, a ^ 2) for a in range(size_f)])
    ys[1] = lax.ppermute(y, "af", [(a, a ^ 1) for a in range(size_f)])
    ys[3] = lax.ppermute(ys[2], "af", [(a, a ^ 1) for a in range(size_f)])
    g = gram(y)
    step = 1
    while step < size_f:
        g = g + lax.ppermute(g, "af", [(a, a ^ step) for a in range(size_f)])
        step *= 2
    step = 1
    while step < size_x:
        g = g + lax.ppermute(g, "gx", [(a, a ^ step) for a in range(size_x)])
        step *= 2
    length = parts * planes * nvar * rad * azi * size_x
    coeff, linv = factor(g, length)
    return basis_of(linv, ys, forcing.shape), coeff


def solution(mesh):
    placed = (
        P("af", None, "gx", None, None, None),
        P("gx", None, None),
        P("gx", None, None),
        P(),
        P(),
    )
    return jax.shard_map(
        functools.partial(on_device, mesh.shape["gx"], mesh.shape["af"]),
        mesh=mesh,
        in_specs=placed,
        out_specs=(P("af", None, "gx", None, None, None), P()),
        check_vma=False,
    )
```

time: 231 us -> 107 us (0.46)
  waiting for transfers between devices: 88.6 us -> 35 us
  starting transfers between devices: 54.9 us -> 25 us
  Pallas kernels: 0 us -> 25.5 us
  blocking collectives: 38.7 us -> 16.3 us
  matrix products: 18.3 us -> 0 us
  other arithmetic: 16 us -> 1.31 us
  local copies, waits for them, and re-layouts: 12.5 us -> 2.27 us
    ppermute x16 -> x15, waiting for transfers between devices: 79.1 us -> 35 us  [the longest x1 16 us: on_device(): ys[2] = lax.ppermute(y, 'af', [(a, a ^ 2) for a in range(size_f)])]
    ppermute x16 -> x15, starting transfers between devices: 51.5 us -> 25 us  [the longest x3 15.6 us: on_device(): mine.append(lax.ppermute(slabs[k], 'gx', pairs))]
    psum x2 -> x0, blocking collectives: 25.9 us -> none  [the longest x1 20.1 us: on_device(): gram = lax.psum(partial_gram, 'gx')]
    pallas_call x0 -> x5, Pallas kernels: none -> 25.5 us  [the longest x1 13.8 us: sweeps(): pl.pallas_call(functools.partial(sweep_kernel, dims, two_sided), out_shap...]
    dot_general x10 -> x0, matrix products: 18.1 us -> none  [the longest x8 16.5 us: apply_adjoint(): jnp.einsum('wv,kpxwrt->kpxvrt', coupling, field, precision=lax.Precision....]
    all_to_all x1 -> x0, waiting for transfers between devices: 9.51 us -> none  [on_device(): lax.all_to_all(scaled.reshape(regrouped.shape), 'af', split_axis=0, conca...]
    slice x22 -> x0, local copies, waits for them, and re-layouts: 5.71 us -> none  [the longest x14 4.12 us: apply_adjoint(): lap = lap + jnp.roll(field, 1, -1) + jnp.roll(field, -1, -1) - 6.0 * field]
    add x9 -> x5, other arithmetic: 6.2 us -> 1.31 us  [the longest x2 0.7 us: on_device(): g = g + lax.ppermute(g, 'af', [(a, a ^ step) for a in range(size_f)])]
  transfers between devices with their start and end apart: 17 -> 15, of which waited for: 17 -> 8; matrix products, arithmetic and copies ran while one was open for 1% -> 1% of each run, Pallas kernels for 0% -> 6%
where the time goes in v1:
time: 107 us; the launch traced here: 106 us
  waiting for transfers between devices  35 us (33%)
  Pallas kernels  25.5 us (24%)
  starting transfers between devices  25 us (23%)
  blocking collectives  16.3 us (15%)
  local copies, waits for them, and re-layouts  2.27 us (2%)
  other arithmetic  1.31 us (1%)
    all_to_all x1, blocking collectives, on_device(): lax.all_to_all(z, ('gx', 'af'), 0, 0, axis_index_groups=together, tiled=T...  16.3 us
    ppermute x1, waiting for transfers between devices, on_device(): ys[2] = lax.ppermute(y, 'af', [(a, a ^ 2) for a in range(size_f)])  16 us
    ppermute x3, starting transfers between devices, on_device(): mine.append(lax.ppermute(slabs[k], 'gx', pairs))  15.6 us
    pallas_call x1, Pallas kernels, sweeps(): pl.pallas_call(functools.partial(sweep_kernel, dims, two_sided), out_shap...  13.8 us
    ppermute x3, waiting for transfers between devices, on_device(): g = g + lax.ppermute(g, 'gx', [(a, a ^ step) for a in range(size_x)])  7.87 us
    ppermute x4, waiting for transfers between devices, on_device(): halo.append(lax.ppermute(slabs[k], 'gx', pairs))  6.73 us
    ppermute x2, waiting for transfers between devices, on_device(): g = g + lax.ppermute(g, 'af', [(a, a ^ step) for a in range(size_f)])  4.21 us
    ppermute x3, starting transfers between devices, on_device(): g = g + lax.ppermute(g, 'gx', [(a, a ^ step) for a in range(size_x)])  3.98 us
  transfers between devices with their start and end apart: 15, of which 8 were waited for; matrix products, arithmetic and copies ran while one was open for 1% of the time, Pallas kernels for 6%

profile of v1, /device:TPU:0, one launch (start us, length us, event | category | flops | bytes accessed | tf_op | source)
XLA Modules:
  0.0 106.2 jit_solution(10288827033721594393)
XLA Ops:
  0.6 2.0 %pack.1 = (f32[48,8,128]{2,1,0:T(8,128)}, f32[48,8,128]{2,1,0:T(8,128)}, f32[48,8,128]{2,1,0:T(8,128)}, f32[48,8,128]{2,1,0:T(8,128)}) custom-call(f32[4,2,4,5,4,256]{5,4,3,2,1,0:T(4,128)} %forcing_ref.1, f32[4,4,256]{2,1,0:T(4,128)} %sponge_ref.1, f32[4,4,256]{2,1,0:T(4,128)} %flow_ref.1), custom_call_target="tpu_custom_call" | custom-call | tf_op jit(solution)/shard_map/pack/pallas_call | solution.py:42
  2.7 1.3 %collective-permute-start.3 = (f32[48,8,128]{2,1,0:T(8,128)}, f32[48,8,128]{2,1,0:T(8,128)S(1)}, u32[]{:S(2)}, u32[]{:S(2)}) collective-permute-start(f32[48,8,128]{2,1,0:T(8,128)} %get-tuple-element.8.refs_2_), channel_id=1, source_target_pairs={{8,24},{12,28},{16,0},{20,4},{9,25},{13,29},{17,1},{21,5},{10,26},... | collective-permute-start | bytes 589832 | tf_op jit(solution)/shard_map/ppermute | solution.py:320
  4.0 0.7 collective-permute-start.4
  4.6 3.6 %collective-permute-start = (f32[48,8,128]{2,1,0:T(8,128)}, f32[48,8,128]{2,1,0:T(8,128)S(1)}, u32[]{:S(2)}, u32[]{:S(2)}) collective-permute-start(f32[48,8,128]{2,1,0:T(8,128)} %get-tuple-element.9), channel_id=1, source_target_pairs={{0,4},{4,8},{8,12},{12,0},{16,20},{20,24},{24,28},{28,16},{1,5},{5... | collective-permute-start | bytes 589832 | tf_op jit(solution)/shard_map/ppermute | solution.py:324
  8.9 8.7 %collective-permute-start.1 = (f32[48,8,128]{2,1,0:T(8,128)}, f32[48,8,128]{2,1,0:T(8,128)S(1)}, u32[]{:S(2)}, u32[]{:S(2)}) collective-permute-start(f32[48,8,128]{2,1,0:T(8,128)} %get-tuple-element.10), channel_id=1, source_target_pairs={{0,8},{4,12},{8,0},{12,4},{16,24},{20,28},{24,16},{28,20},{1,9},{5... | collective-permute-start | bytes 589832 | tf_op jit(solution)/shard_map/ppermute | solution.py:324
  17.7 1.3 %collective-permute-start.6 = (f32[48,8,128]{2,1,0:T(8,128)}, f32[48,8,128]{2,1,0:T(8,128)S(1)}, u32[]{:S(2)}, u32[]{:S(2)}) collective-permute-start(f32[48,8,128]{2,1,0:T(8,128)} %get-tuple-element.11), channel_id=1, source_target_pairs={{8,20},{12,24},{16,12},{20,0},{9,21},{13,25},{17,13},{21,1},{10,22... | collective-permute-start | bytes 589832 | tf_op jit(solution)/shard_map/ppermute | solution.py:320
  19.0 3.2 %collective-permute-start.2 = (f32[48,8,128]{2,1,0:T(8,128)}, f32[48,8,128]{2,1,0:T(8,128)S(1)}, u32[]{:S(2)}, u32[]{:S(2)}) collective-permute-start(f32[48,8,128]{2,1,0:T(8,128)} %get-tuple-element.11), channel_id=1, source_target_pairs={{0,12},{4,0},{8,4},{12,8},{16,28},{20,16},{24,20},{28,24},{1,13},{... | collective-permute-start | bytes 589832 | tf_op jit(solution)/shard_map/ppermute | solution.py:324
  22.2 6.7 %collective-permute-done.6.refs_9_ = f32[48,8,128]{2,1,0:T(8,128)S(1)} collective-permute-done((f32[48,8,128]{2,1,0:T(8,128)}, f32[48,8,128]{2,1,0:T(8,128)S(1)}, u32[]{:S(2)}, u32[]{:S(2)}) %collective-permute-start.6) | collective-permute-done | bytes 196640 | tf_op jit(solution)/shard_map/ppermute | solution.py:320
  29.7 0.7 copy-done.10
  30.3 13.8 %sweeps.1 = f32[16,10,8,128]{3,2,1,0:T(8,128)} custom-call(f32[5,5]{1,0:T(8,128)} %refs_0_.1, f32[2]{0:T(128)} %refs_1_.1, f32[48,8,128]{2,1,0:T(8,128)} %get-tuple-element.8.refs_2_, f32[48,8,128]{2,1,0:T(8,128)} %copy-done.6, f32[48,8,128]{2,1,0:T(8,128)} %copy-done.8, f32[48,8,128]{2,1,0:T(8,128)} %copy-done.10, f32[48,8,128]{2,1,0:T(8,128)} %copy-done.4, ...), custom_call_target="tpu_custom_call" | custom-call | tf_op jit(solution)/shard_map/sweeps/pallas_call | solution.py:188
  44.1 16.3 %all_to_all.5.y_ref.refs_0_ = f32[16,10,8,128]{3,2,1,0:T(8,128)S(1)} all-to-all(f32[16,10,8,128]{3,2,1,0:T(8,128)} %sweeps.1), channel_id=1, replica_groups={{0,4,8,12,1,5,9,13,2,6,10,14,3,7,11,15},{16,20,24,28,17,21,25,29,18,22,..., dimensions={0} | all-to-all | bytes 1310720 | tf_op jit(solution)/shard_map/all_to_all | solution.py:330
  60.4 0.7 collective-permute-start.13
  61.2 16.0 %collective-permute-done.13.refs_2_ = f32[16,10,8,128]{3,2,1,0:T(8,128)S(1)} collective-permute-done((f32[16,10,8,128]{3,2,1,0:T(8,128)S(1)}, f32[16,10,8,128]{3,2,1,0:T(8,128)S(1)}, u32[]{:S(2)}, u32[]{:S(2)}) %collective-permute-start.13) | collective-permute-done | bytes 655392 | tf_op jit(solution)/shard_map/ppermute | solution.py:332
  77.2 3.8 %gram.1 = f32[16,16]{1,0:T(8,128)} custom-call(f32[16,10,8,128]{3,2,1,0:T(8,128)} %copy-done), custom_call_target="tpu_custom_call" | custom-call | tf_op jit(solution)/shard_map/gram/pallas_call | solution.py:226
  81.3 1.1 %collective-permute-done.7 = f32[16,16]{1,0:T(8,128)S(1)} collective-permute-done((f32[16,16]{1,0:T(8,128)}, f32[16,16]{1,0:T(8,128)S(1)}, u32[]{:S(2)}, u32[]{:S(2)}) %collective-permute-start.7) | collective-permute-done | bytes 1056 | tf_op jit(solution)/shard_map/ppermute | solution.py:338
  82.4 0.7 add.15
  83.6 3.1 %collective-permute-done.8 = f32[16,16]{1,0:T(8,128)S(1)} collective-permute-done((f32[16,16]{1,0:T(8,128)S(1)}, f32[16,16]{1,0:T(8,128)S(1)}, u32[]{:S(2)}, u32[]{:S(2)}) %collective-permute-start.8) | collective-permute-done | bytes 1056 | tf_op jit(solution)/shard_map/ppermute | solution.py:338
  87.3 3.1 %collective-permute-done.9 = f32[16,16]{1,0:T(8,128)S(1)} collective-permute-done((f32[16,16]{1,0:T(8,128)S(1)}, f32[16,16]{1,0:T(8,128)S(1)}, u32[]{:S(2)}, u32[]{:S(2)}) %collective-permute-start.9) | collective-permute-done | bytes 1056 | tf_op jit(solution)/shard_map/ppermute | solution.py:342
  91.0 3.0 %collective-permute-done.10 = f32[16,16]{1,0:T(8,128)S(1)} collective-permute-done((f32[16,16]{1,0:T(8,128)S(1)}, f32[16,16]{1,0:T(8,128)S(1)}, u32[]{:S(2)}, u32[]{:S(2)}) %collective-permute-start.10) | collective-permute-done | bytes 1056 | tf_op jit(solution)/shard_map/ppermute | solution.py:342
  94.1 2.8 %collective-permute-start.11 = (f32[16,16]{1,0:T(8,128)S(1)}, f32[16,16]{1,0:T(8,128)S(1)}, u32[]{:S(2)}, u32[]{:S(2)}) collective-permute-start(f32[16,16]{1,0:T(8,128)S(1)} %add.18), channel_id=1, source_target_pairs={{0,16},{4,20},{8,24},{12,28},{16,0},{20,4},{24,8},{28,12},{1,17},{... | collective-permute-start | bytes 3080 | tf_op jit(solution)/shard_map/ppermute | solution.py:342
  96.8 1.8 %collective-permute-done.11 = f32[16,16]{1,0:T(8,128)S(1)} collective-permute-done((f32[16,16]{1,0:T(8,128)S(1)}, f32[16,16]{1,0:T(8,128)S(1)}, u32[]{:S(2)}, u32[]{:S(2)}) %collective-permute-start.11) | collective-permute-done | bytes 1056 | tf_op jit(solution)/shard_map/ppermute | solution.py:342
  99.2 2.6 %factor.1 = (f32[16,16]{1,0:T(8,128)}, f32[16,16]{1,0:T(8,128)}) custom-call(f32[16,16]{1,0:T(8,128)} %add.19.g_ref), custom_call_target="tpu_custom_call" | custom-call | tf_op jit(solution)/shard_map/factor/pallas_call | solution.py:256
  101.8 0.8 copy-done.2
  102.8 3.4 %basis.1 = f32[4,2,4,5,4,256]{5,4,3,2,1,0:T(4,128)} custom-call(f32[16,16]{1,0:T(8,128)} %get-tuple-element.12.linv_ref, f32[16,10,8,128]{3,2,1,0:T(8,128)} %copy-done, f32[16,10,8,128]{3,2,1,0:T(8,128)} %copy-done.2, f32[16,10,8,128]{3,2,1,0:T(8,128)} %copy-done.1, f32[16,10,8,128]{3,2,1,0:T(8,128)} %copy-done.3), custom_call_target="tpu_custom_call" | custom-call | tf_op jit(solution)/shard_map/basis/pallas_call | solution.py:292
  (39 shorter events, 4.2 us)
Async XLA Ops:
  2.7 15.0 %collective-permute-start.3 = (f32[48,8,128]{2,1,0:T(8,128)}, f32[48,8,128]{2,1,0:T(8,128)S(1)}, u32[]{:S(2)}, u32[]{:S(2)}) collective-permute-start(f32[48,8,128]{2,1,0:T(8,128)} %get-tuple-element.8.refs_2_), channel_id=1, source_target_pairs={{8,24},{12,28},{16,0},{20,4},{9,25},{13,29},{17,1},{21,5},{10,26},... | collective-permute-start | bytes 589832 | tf_op jit(solution)/shard_map/ppermute | solution.py:320
  4.0 15.0 %collective-permute-start.4 = (f32[48,8,128]{2,1,0:T(8,128)}, f32[48,8,128]{2,1,0:T(8,128)S(1)}, u32[]{:S(2)}, u32[]{:S(2)}) collective-permute-start(f32[48,8,128]{2,1,0:T(8,128)} %get-tuple-element.9), channel_id=1, source_target_pairs={{8,28},{12,16},{16,4},{20,8},{9,29},{13,17},{17,5},{21,9},{10,30},... | collective-permute-start | bytes 589832 | tf_op jit(solution)/shard_map/ppermute | solution.py:320
  4.6 17.6 %collective-permute-start = (f32[48,8,128]{2,1,0:T(8,128)}, f32[48,8,128]{2,1,0:T(8,128)S(1)}, u32[]{:S(2)}, u32[]{:S(2)}) collective-permute-start(f32[48,8,128]{2,1,0:T(8,128)} %get-tuple-element.9), channel_id=1, source_target_pairs={{0,4},{4,8},{8,12},{12,0},{16,20},{20,24},{24,28},{28,16},{1,5},{5... | collective-permute-start | bytes 589832 | tf_op jit(solution)/shard_map/ppermute | solution.py:324
  8.3 13.9 %collective-permute-start.5 = (f32[48,8,128]{2,1,0:T(8,128)}, f32[48,8,128]{2,1,0:T(8,128)S(1)}, u32[]{:S(2)}, u32[]{:S(2)}) collective-permute-start(f32[48,8,128]{2,1,0:T(8,128)} %get-tuple-element.10), channel_id=1, source_target_pairs={{8,16},{12,20},{16,8},{20,12},{9,17},{13,21},{17,9},{21,13},{10,18... | collective-permute-start | bytes 589832 | tf_op jit(solution)/shard_map/ppermute | solution.py:320
  8.9 13.3 %collective-permute-start.1 = (f32[48,8,128]{2,1,0:T(8,128)}, f32[48,8,128]{2,1,0:T(8,128)S(1)}, u32[]{:S(2)}, u32[]{:S(2)}) collective-permute-start(f32[48,8,128]{2,1,0:T(8,128)} %get-tuple-element.10), channel_id=1, source_target_pairs={{0,8},{4,12},{8,0},{12,4},{16,24},{20,28},{24,16},{28,20},{1,9},{5... | collective-permute-start | bytes 589832 | tf_op jit(solution)/shard_map/ppermute | solution.py:324
  17.7 11.5 %copy-start.4 = (f32[48,8,128]{2,1,0:T(8,128)}, f32[48,8,128]{2,1,0:T(8,128)S(1)}, u32[]{:S(2)}) copy-start(f32[48,8,128]{2,1,0:T(8,128)S(1)} %collective-permute-done.3.refs_6_) | copy-start | bytes 589828
  17.7 11.3 %collective-permute-start.6 = (f32[48,8,128]{2,1,0:T(8,128)}, f32[48,8,128]{2,1,0:T(8,128)S(1)}, u32[]{:S(2)}, u32[]{:S(2)}) collective-permute-start(f32[48,8,128]{2,1,0:T(8,128)} %get-tuple-element.11), channel_id=1, source_target_pairs={{8,20},{12,24},{16,12},{20,0},{9,21},{13,25},{17,13},{21,1},{10,22... | collective-permute-start | bytes 589832 | tf_op jit(solution)/shard_map/ppermute | solution.py:320
  19.0 10.2 %copy-start.5 = (f32[48,8,128]{2,1,0:T(8,128)}, f32[48,8,128]{2,1,0:T(8,128)S(1)}, u32[]{:S(2)}) copy-start(f32[48,8,128]{2,1,0:T(8,128)S(1)} %collective-permute-done.4.refs_7_) | copy-start | bytes 589828
  19.0 10.1 %collective-permute-start.2 = (f32[48,8,128]{2,1,0:T(8,128)}, f32[48,8,128]{2,1,0:T(8,128)S(1)}, u32[]{:S(2)}, u32[]{:S(2)}) collective-permute-start(f32[48,8,128]{2,1,0:T(8,128)} %get-tuple-element.11), channel_id=1, source_target_pairs={{0,12},{4,0},{8,4},{12,8},{16,28},{20,16},{24,20},{28,24},{1,13},{... | collective-permute-start | bytes 589832 | tf_op jit(solution)/shard_map/ppermute | solution.py:324
  22.2 6.9 %copy-start.6 = (f32[48,8,128]{2,1,0:T(8,128)}, f32[48,8,128]{2,1,0:T(8,128)S(1)}, u32[]{:S(2)}) copy-start(f32[48,8,128]{2,1,0:T(8,128)S(1)} %collective-permute-done.refs_3_) | copy-start | bytes 589828
  22.2 6.9 %copy-start.7 = (f32[48,8,128]{2,1,0:T(8,128)}, f32[48,8,128]{2,1,0:T(8,128)S(1)}, u32[]{:S(2)}) copy-start(f32[48,8,128]{2,1,0:T(8,128)S(1)} %collective-permute-done.5.refs_8_) | copy-start | bytes 589828
  22.2 6.9 %copy-start.8 = (f32[48,8,128]{2,1,0:T(8,128)}, f32[48,8,128]{2,1,0:T(8,128)S(1)}, u32[]{:S(2)}) copy-start(f32[48,8,128]{2,1,0:T(8,128)S(1)} %collective-permute-done.1.refs_4_) | copy-start | bytes 589828
  60.4 16.8 %copy-start = (f32[16,10,8,128]{3,2,1,0:T(8,128)}, f32[16,10,8,128]{3,2,1,0:T(8,128)S(1)}, u32[]{:S(2)}) copy-start(f32[16,10,8,128]{3,2,1,0:T(8,128)S(1)} %all_to_all.5.y_ref.refs_0_) | copy-start | bytes 1966084
  60.4 16.8 %collective-permute-start.13 = (f32[16,10,8,128]{3,2,1,0:T(8,128)S(1)}, f32[16,10,8,128]{3,2,1,0:T(8,128)S(1)}, u32[]{:S(2)}, u32[]{:S(2)}) collective-permute-start(f32[16,10,8,128]{3,2,1,0:T(8,128)S(1)} %all_to_all.5.y_ref.refs_0_), channel_id=1, source_target_pairs={{0,2},{1,3},{2,0},{3,1},{4,6},{5,7},{6,4},{7,5},{8,10},{9,11},{10,... | collective-permute-start | bytes 1966088 | tf_op jit(solution)/shard_map/ppermute | solution.py:332
  61.2 40.6 %collective-permute-start.12 = (f32[16,10,8,128]{3,2,1,0:T(8,128)S(1)}, f32[16,10,8,128]{3,2,1,0:T(8,128)S(1)}, u32[]{:S(2)}, u32[]{:S(2)}) collective-permute-start(f32[16,10,8,128]{3,2,1,0:T(8,128)S(1)} %all_to_all.5.y_ref.refs_0_), channel_id=1, source_target_pairs={{0,1},{1,0},{2,3},{3,2},{4,5},{5,4},{6,7},{7,6},{8,9},{9,8},{10,11... | collective-permute-start | bytes 1966088 | tf_op jit(solution)/shard_map/ppermute | solution.py:333
  77.2 24.6 %copy-start.1 = (f32[16,10,8,128]{3,2,1,0:T(8,128)}, f32[16,10,8,128]{3,2,1,0:T(8,128)S(1)}, u32[]{:S(2)}) copy-start(f32[16,10,8,128]{3,2,1,0:T(8,128)S(1)} %collective-permute-done.13.refs_2_) | copy-start | bytes 1966084
  77.2 24.6 %collective-permute-start.14 = (f32[16,10,8,128]{3,2,1,0:T(8,128)S(1)}, f32[16,10,8,128]{3,2,1,0:T(8,128)S(1)}, u32[]{:S(2)}, u32[]{:S(2)}) collective-permute-start(f32[16,10,8,128]{3,2,1,0:T(8,128)S(1)} %collective-permute-done.13.refs_2_), channel_id=1, source_target_pairs={{0,1},{1,0},{2,3},{3,2},{4,5},{5,4},{6,7},{7,6},{8,9},{9,8},{10,11... | collective-permute-start | bytes 1966088 | tf_op jit(solution)/shard_map/ppermute | solution.py:334
  81.0 1.4 %collective-permute-start.7 = (f32[16,16]{1,0:T(8,128)}, f32[16,16]{1,0:T(8,128)S(1)}, u32[]{:S(2)}, u32[]{:S(2)}) collective-permute-start(f32[16,16]{1,0:T(8,128)} %gram.1), channel_id=1, source_target_pairs={{0,1},{1,0},{2,3},{3,2},{4,5},{5,4},{6,7},{7,6},{8,9},{9,8},{10,11... | collective-permute-start | bytes 3080 | tf_op jit(solution)/shard_map/ppermute | solution.py:338
  83.1 3.7 %collective-permute-start.8 = (f32[16,16]{1,0:T(8,128)S(1)}, f32[16,16]{1,0:T(8,128)S(1)}, u32[]{:S(2)}, u32[]{:S(2)}) collective-permute-start(f32[16,16]{1,0:T(8,128)S(1)} %add.15), channel_id=1, source_target_pairs={{0,2},{1,3},{2,0},{3,1},{4,6},{5,7},{6,4},{7,5},{8,10},{9,11},{10,... | collective-permute-start | bytes 3080 | tf_op jit(solution)/shard_map/ppermute | solution.py:338
  86.7 3.7 %collective-permute-start.9 = (f32[16,16]{1,0:T(8,128)S(1)}, f32[16,16]{1,0:T(8,128)S(1)}, u32[]{:S(2)}, u32[]{:S(2)}) collective-permute-start(f32[16,16]{1,0:T(8,128)S(1)} %add.16), channel_id=1, source_target_pairs={{0,4},{4,0},{8,12},{12,8},{16,20},{20,16},{24,28},{28,24},{1,5},{5... | collective-permute-start | bytes 3080 | tf_op jit(solution)/shard_map/ppermute | solution.py:342
  90.4 3.7 %collective-permute-start.10 = (f32[16,16]{1,0:T(8,128)S(1)}, f32[16,16]{1,0:T(8,128)S(1)}, u32[]{:S(2)}, u32[]{:S(2)}) collective-permute-start(f32[16,16]{1,0:T(8,128)S(1)} %add.17), channel_id=1, source_target_pairs={{0,8},{4,12},{8,0},{12,4},{16,24},{20,28},{24,16},{28,20},{1,9},{5... | collective-permute-start | bytes 3080 | tf_op jit(solution)/shard_map/ppermute | solution.py:342
  94.1 4.5 %collective-permute-start.11 = (f32[16,16]{1,0:T(8,128)S(1)}, f32[16,16]{1,0:T(8,128)S(1)}, u32[]{:S(2)}, u32[]{:S(2)}) collective-permute-start(f32[16,16]{1,0:T(8,128)S(1)} %add.18), channel_id=1, source_target_pairs={{0,16},{4,20},{8,24},{12,28},{16,0},{20,4},{24,8},{28,12},{1,17},{... | collective-permute-start | bytes 3080 | tf_op jit(solution)/shard_map/ppermute | solution.py:342
  101.8 0.9 copy-start.2
  101.8 1.1 %copy-start.3 = (f32[16,10,8,128]{3,2,1,0:T(8,128)}, f32[16,10,8,128]{3,2,1,0:T(8,128)S(1)}, u32[]{:S(2)}) copy-start(f32[16,10,8,128]{3,2,1,0:T(8,128)S(1)} %collective-permute-done.14.refs_3_) | copy-start | bytes 1966084
  (2 other events, 1.4 us)

commit v2 on v1

--- a/solution.py
+++ b/solution.py
@@ -19,20 +19,33 @@
     return jnp.concatenate([plane[:, :LANE], plane[:, LANE:]], axis=0)
 
 
-def pack_kernel(forcing_ref, sponge_ref, flow_ref, *out_refs):
-    cols, parts, planes, nvar = forcing_ref.shape[:4]
+def pack_kernel(forcing_hbm, sponge_hbm, flow_hbm, *refs):
+    cols, parts, planes, nvar = forcing_hbm.shape[:4]
+    out_refs, (forcing_ref, sponge_ref, flow_ref, sems) = refs[:cols], refs[cols:]
     me = lax.rem(lax.axis_index("gx"), cols)
     rows = parts * planes * nvar
+    copies = []
+    for k in range(cols):
+        col = lax.rem(me + k, cols)
+        copies.append(pltpu.make_async_copy(forcing_hbm.at[col], forcing_ref.at[k], sems.at[k]))
+    copies.append(pltpu.make_async_copy(sponge_hbm, sponge_ref, sems.at[cols]))
+    copies.append(pltpu.make_async_copy(flow_hbm, flow_ref, sems.at[cols + 1]))
+    for copy in copies:
+        copy.start()
+    for copy in copies[cols:]:
+        copy.wait()
+    for plane in range(planes):
+        sponge, flow = fold(sponge_ref[plane]), fold(flow_ref[plane])
+        for out_ref in out_refs:
+            out_ref[rows + plane] = sponge
+            out_ref[rows + planes + plane] = flow
     for k, out_ref in enumerate(out_refs):
-        col = lax.rem(me + k, cols)
+        copies[k].wait()
         for part in range(parts):
             for plane in range(planes):
                 for v in range(nvar):
                     row = (part * planes + plane) * nvar + v
-                    out_ref[row] = fold(forcing_ref[col, part, plane, v])
-        for plane in range(planes):
-            out_ref[rows + plane] = fold(sponge_ref[plane])
-            out_ref[rows + planes + plane] = fold(flow_ref[plane])
+                    out_ref[row] = fold(forcing_ref[k, part, plane, v])
 
 
 def pack(forcing, sponge, flow):
@@ -42,67 +55,78 @@
     return pl.pallas_call(
         pack_kernel,
         out_shape=(slab,) * cols,
-        in_specs=[pl.BlockSpec(memory_space=pltpu.VMEM)] * 3,
+        in_specs=[pl.BlockSpec(memory_space=pltpu.HBM)] * 3,
         out_specs=(pl.BlockSpec(memory_space=pltpu.VMEM),) * cols,
+        scratch_shapes=[
+            pltpu.VMEM(forcing.shape, jnp.float32),
+            pltpu.VMEM(sponge.shape, jnp.float32),
+            pltpu.VMEM(flow.shape, jnp.float32),
+            pltpu.SemaphoreType.DMA((cols + 2,)),
+        ],
+        compiler_params=pltpu.CompilerParams(vmem_limit_bytes=4 << 20),
         name="pack",
     )(forcing, sponge, flow)
 
 
-def locate(i, two_sided, flip, cols, planes, span):
-    own = cols * planes
-    if two_sided:
-        j = i - span
-        slab, inner = lax.div(j + span, planes) - span // planes, lax.rem(i, planes)
-        slot = jnp.where(slab < 0, slab + 2 * cols, slab)
-        return slot, inner, i
-    slab, inner = lax.div(i, planes), lax.rem(i, planes)
-    far = jnp.where(i < own, cols - 1 - slab, 3 * cols - 1 - slab)
-    return jnp.where(flip == 1, far, slab), jnp.where(flip == 1, planes - 1 - inner, inner), i
-
-
-def sweep_kernel(dims, two_sided, *refs):
+def sweep_kernel(dims, two_sided, outer, *refs):
     cols, parts, planes, nvar, groups = dims
-    coupling_ref, omega_ref = refs[:2]
-    slab_refs = refs[2 : 2 + 2 * cols]
-    out_ref = refs[2 + 2 * cols]
-    raw, first, even, odd, p_re, p_im, w_lo, w_hi, sems = refs[3 + 2 * cols :]
+    comp = parts * nvar
+    state = 8
+    coupling_hbm, omega_hbm = refs[:2]
+    slab_refs = refs[2 : 2 + cols]
+    at = 2 + cols + (state if outer else 0)
+    out_ref, first, even, odd, p_re, p_im, w_lo, w_hi = refs[at : at + state]
+    raw, coupling_ref, omega_ref, sems = refs[at + state :]
     gx = lax.axis_index("gx")
     me, group = lax.rem(gx, cols), lax.div(gx, cols)
     flip = jnp.int32(0) if two_sided else jnp.int32(group)
-    rows = planes * (parts * nvar + 2)
-    comp = parts * nvar
+    rows = planes * (comp + 2)
     own, span = cols * planes, SWEEPS
-    window = own + span * (2 if two_sided else 1)
-
+    begin = span if two_sided else 0
+    end = begin + own
+    window = end + span
+
+    scalars = [
+        pltpu.make_async_copy(coupling_hbm, coupling_ref, sems.at[cols]),
+        pltpu.make_async_copy(omega_hbm, omega_ref, sems.at[cols + 1]),
+    ]
+    for copy in scalars:
+        copy.start()
     copies = []
     for k, slab_ref in enumerate(slab_refs):
-        slot = lax.rem(me + cols - k % cols, cols) + cols * (k // cols)
+        slot = lax.rem(me + cols - k, cols)
         copies.append(pltpu.make_async_copy(slab_ref, raw.at[pl.ds(slot * rows, rows)], sems.at[k]))
         copies[-1].start()
 
+    for copy in scalars:
+        copy.wait()
     column = lax.axis_index("af") * cols + me
     freq = jnp.where(column < FORCINGS, omega_ref[0], omega_ref[1])
     side = jnp.where(flip == 1, -2.0, 2.0).astype(jnp.float32)
-    zero = jnp.zeros((SUB, LANE), jnp.float32)
-    for ref in (first, even, odd):
-        for c in range(comp):
-            ref[c] = zero
+    if not outer:
+        for ref in (first, even, odd):
+            for c in range(comp):
+                ref[c] = jnp.zeros((SUB, LANE), jnp.float32)
     for copy in copies:
         copy.wait()
 
     def prepare(i, _):
-        slot, inner, _ = locate(i, two_sided, flip, cols, planes, span)
+        slab, inner = lax.div(i - begin + span, planes) - span // planes, lax.rem(i, planes)
+        if two_sided:
+            slot = jnp.where(slab < 0, slab + cols, lax.rem(slab, cols))
+            inside = jnp.logical_and(
+                jnp.logical_or(i >= begin, group > 0), jnp.logical_or(i < end, group < groups - 1)
+            )
+            keep = jnp.where(inside, 1.0, 0.0).astype(jnp.float32)
+        else:
+            slot = lax.rem(slab, cols)
+            slot = jnp.where(flip == 1, cols - 1 - slot, slot)
+            inner = jnp.where(flip == 1, planes - 1 - inner, inner)
         base = slot * rows
         sponge = raw[base + planes * comp + inner]
         flow = raw[base + planes * comp + planes + inner]
         w_lo[i] = 1.0 - side * flow
         w_hi[i] = 1.0 + side * flow
-        if two_sided:
-            inside = jnp.logical_and(
-                jnp.logical_or(i >= span, group > 0),
-                jnp.logical_or(i < span + own, group < groups - 1),
-            )
-            keep = jnp.where(inside, 1.0, 0.0).astype(jnp.float32)
         for v in range(nvar):
             diag = sponge + (6.0 * viscosity - coupling_ref[v, v])
             scale = 1.0 / (diag * diag + freq * freq)
@@ -117,7 +141,12 @@
             p_im[i * nvar + v] = viscosity * pi
         return 0
 
-    lax.fori_loop(0, window, prepare, 0)
+    if outer:
+        lax.fori_loop(end, window, prepare, 0)
+        if two_sided:
+            lax.fori_loop(0, begin, prepare, 0)
+    else:
+        lax.fori_loop(begin, end, prepare, 0)
 
     lane = lax.broadcasted_iota(jnp.int32, (SUB, LANE), 1)
     radial = lax.rem(lax.broadcasted_iota(jnp.int32, (SUB, LANE), 0), SUB // 2)
@@ -148,7 +177,7 @@
             emit(i, v, first[(i + 1) * comp + v] + (pr * sums[0] - pi * sums[1]))
             emit(i, nvar + v, first[(i + 1) * comp + nvar + v] + (pr * sums[1] + pi * sums[0]))
 
-    def level(src, emit, lo, hi, unroll):
+    def level(src, emit, lo, hi, unroll=2):
         def body(n, _):
             for m in range(unroll):
                 update(lo + n * unroll + m, src, emit)
@@ -166,43 +195,50 @@
         return emit
 
     def finish(i, c, value):
-        plane = i - span if two_sided else jnp.where(flip == 1, own - 1 - i, i)
+        plane = i - begin if two_sided else jnp.where(flip == 1, own - 1 - i, i)
         out_ref[lax.rem(plane, planes) * cols + lax.div(plane, planes), c] = value
 
     src = first
-    for s in range(1, SWEEPS):
+    for s in range(1, SWEEPS + 1):
         dst = odd if s % 2 else even
-        level(src, into(dst), s if two_sided else 0, window - s, 2)
+        emit = finish if s == SWEEPS else into(dst)
+        if outer:
+            if two_sided:
+                level(src, emit, s, begin + s)
+            level(src, emit, end - s, window - s)
+        else:
+            level(src, emit, begin + s if two_sided else 0, end - s)
         src = dst
-    start = span if two_sided else 0
-    level(src, finish, start, start + own, 2)
-
-
-def sweeps(coupling, omega, slabs, dims, two_sided):
+
+
+def sweeps(coupling, omega, slabs, dims, two_sided, state=()):
     cols, parts, planes, nvar, groups = dims
     comp = parts * nvar
-    rows = planes * (comp + 2)
     own = cols * planes
     window = own + SWEEPS * (2 if two_sided else 1)
-    tiles = lambda n: pltpu.VMEM((n, SUB, LANE), jnp.float32)
+    tiles = lambda n: jax.ShapeDtypeStruct((n, SUB, LANE), jnp.float32)
+    shapes = [jax.ShapeDtypeStruct((own, comp, SUB, LANE), jnp.float32)]
+    shapes += [tiles((window + 2) * comp)] * 3 + [tiles(window * nvar)] * 2 + [tiles(window)] * 2
+    fast = pl.BlockSpec(memory_space=pltpu.VMEM)
+    lead = 2 + len(slabs)
     return pl.pallas_call(
-        functools.partial(sweep_kernel, dims, two_sided),
-        out_shape=jax.ShapeDtypeStruct((own, comp, SUB, LANE), jnp.float32),
-        in_specs=[pl.BlockSpec(memory_space=pltpu.SMEM)] * 2 + [pl.BlockSpec(memory_space=pl.ANY)] * len(slabs),
-        out_specs=pl.BlockSpec(memory_space=pltpu.VMEM),
+        functools.partial(sweep_kernel, dims, two_sided, bool(state)),
+        out_shape=shapes,
+        in_specs=[pl.BlockSpec(memory_space=pltpu.HBM)] * 2
+        + [pl.BlockSpec(memory_space=pl.ANY)] * len(slabs)
+        + [fast] * len(state),
+        out_specs=[fast] * len(shapes),
         scratch_shapes=[
-            tiles(2 * cols * rows),
-            tiles((window + 2) * comp),
-            tiles((window + 2) * comp),
-            tiles((window + 2) * comp),
-            tiles(window * nvar),
-            tiles(window * nvar),
-            tiles(window),
-            tiles(window),
-            pltpu.SemaphoreType.DMA((2 * cols,)),
+            pltpu.VMEM((cols * planes * (comp + 2), SUB, LANE), jnp.float32),
+            pltpu.SMEM(coupling.shape, jnp.float32),
+            pltpu.SMEM(omega.shape, jnp.float32),
+            pltpu.SemaphoreType.DMA((cols + 2,)),
         ],
-        name="sweeps",
-    )(coupling, omega, *slabs)
+        input_output_aliases={lead + n: n for n in range(len(state))},
+        compiler_params=pltpu.CompilerParams(vmem_limit_bytes=16 << 20),
+        cost_estimate=pl.CostEstimate(flops=6_000_000_000, bytes_accessed=1 << 20, transcendentals=0),
+        name="outer" if state else "inner",
+    )(coupling, omega, *slabs, *state)
 
 
 def gram_kernel(y_ref, g_ref):
@@ -228,6 +264,8 @@
         out_shape=jax.ShapeDtypeStruct((y.shape[0],) * 2, jnp.float32),
         in_specs=[pl.BlockSpec(memory_space=pltpu.VMEM)],
         out_specs=pl.BlockSpec(memory_space=pltpu.VMEM),
+        compiler_params=pltpu.CompilerParams(vmem_limit_bytes=4 << 20),
+        cost_estimate=pl.CostEstimate(flops=2_000_000_000, bytes_accessed=1 << 20, transcendentals=0),
         name="gram",
     )(y)
 
@@ -258,6 +296,7 @@
         out_shape=(square, square),
         in_specs=[pl.BlockSpec(memory_space=pltpu.VMEM)],
         out_specs=(pl.BlockSpec(memory_space=pltpu.VMEM),) * 2,
+        compiler_params=pltpu.CompilerParams(vmem_limit_bytes=1 << 20),
         name="factor",
     )(g)
 
@@ -295,6 +334,7 @@
         in_specs=[pl.BlockSpec(memory_space=pltpu.VMEM)] * (1 + len(ys)),
         out_specs=pl.BlockSpec(memory_space=pltpu.VMEM),
         scratch_shapes=[pltpu.VMEM((shape[0] * linv.shape[0], SUB, LANE), jnp.float32)],
+        compiler_params=pltpu.CompilerParams(vmem_limit_bytes=8 << 20),
         name="basis",
     )(linv, *ys)
 
@@ -322,7 +362,8 @@
     for k in range(1, cols):
         pairs = [(g, g // cols * cols + (g + k) % cols) for g in range(size_x)]
         mine.append(lax.ppermute(slabs[k], "gx", pairs))
-    z = sweeps(coupling, omega, mine + halo, dims, two_sided)
+    state = sweeps(coupling, omega, mine, dims, two_sided)
+    z = sweeps(coupling, omega, halo, dims, two_sided, state)[0]
 
     together = [
         [(q * cols + j) * size_f + a for a in range(size_f) for j in range(cols)] for q in range(groups)
@@ -331,16 +372,15 @@
     ys = [y] + [None] * (size_f - 1)
     ys[2] = lax.ppermute(y, "af", [(a, a ^ 2) for a in range(size_f)])
     ys[1] = lax.ppermute(y, "af", [(a, a ^ 1) for a in range(size_f)])
-    ys[3] = lax.ppermute(ys[2], "af", [(a, a ^ 1) for a in range(size_f)])
     g = gram(y)
-    step = 1
-    while step < size_f:
-        g = g + lax.ppermute(g, "af", [(a, a ^ step) for a in range(size_f)])
-        step *= 2
     step = 1
     while step < size_x:
         g = g + lax.ppermute(g, "gx", [(a, a ^ step) for a in range(size_x)])
         step *= 2
+    g = g + lax.ppermute(g, "af", [(a, a ^ 1) for a in range(size_f)])
+    g, ys[2] = lax.optimization_barrier((g, ys[2]))
+    g = g + lax.ppermute(g, "af", [(a, a ^ 2) for a in range(size_f)])
+    ys[3] = lax.ppermute(ys[2], "af", [(a, a ^ 1) for a in range(size_f)])
     length = parts * planes * nvar * rad * azi * size_x
     coeff, linv = factor(g, length)
     return basis_of(linv, ys, forcing.shape), coeff

time: 107 us -> 78 us (0.73)
  waiting for transfers between devices: 35 us -> 21.5 us
  starting transfers between devices: 25 us -> 15.2 us
  Pallas kernels: 25.5 us -> 20 us
  local copies, waits for them, and re-layouts: 2.27 us -> 3.85 us
  other arithmetic: 1.31 us -> 0.02 us
    ppermute x1, waiting for transfers between devices: 16 us -> 1.1 us  [on_device(): ys[2] = lax.ppermute(y, 'af', [(a, a ^ 2) for a in range(size_f)])]
    ppermute x3, starting transfers between devices: 15.6 us -> 6.03 us  [on_device(): mine.append(lax.ppermute(slabs[k], 'gx', pairs))]
    ppermute x3, waiting for transfers between devices: 0.15 us -> 5.61 us  [on_device(): mine.append(lax.ppermute(slabs[k], 'gx', pairs))]
    ppermute x4, waiting for transfers between devices: 6.73 us -> 2.59 us  [on_device(): halo.append(lax.ppermute(slabs[k], 'gx', pairs))]
    pallas_call x1, Pallas kernels: 3.79 us -> 1.84 us  [gram(): pl.pallas_call(gram_kernel, out_shape=jax.ShapeDtypeStruct((y.shape[0],)...]
    pallas_call x1, Pallas kernels: 3.36 us -> 1.68 us  [basis_of(): pl.pallas_call(basis_kernel, out_shape=jax.ShapeDtypeStruct(shape, jnp.fl...]
    unnamed x22 -> x10, local copies, waits for them, and re-layouts: 2.27 us -> 3.85 us
    pallas_call x1, Pallas kernels: 2.04 us -> 0.97 us  [pack(): pl.pallas_call(pack_kernel, out_shape=(slab,) * cols, in_specs=[pl.BlockS...]
  transfers between devices with their start and end apart: 15 -> 15, of which waited for: 8 -> 9; matrix products, arithmetic and copies ran while one was open for 1% -> 0% of each run, Pallas kernels for 6% -> 15%
where the time goes in v2:
time: 78 us; the launch traced here: 77.6 us
  waiting for transfers between devices  21.5 us (28%)
  Pallas kernels  20 us (26%)
  blocking collectives  16.3 us (21%)
  starting transfers between devices  15.2 us (19%)
  local copies, waits for them, and re-layouts  3.85 us (5%)
    all_to_all x1, blocking collectives, on_device(): lax.all_to_all(z, ('gx', 'af'), 0, 0, axis_index_groups=together, tiled=T...  16.3 us
    pallas_call x2, Pallas kernels, sweeps(): pl.pallas_call(functools.partial(sweep_kernel, dims, two_sided, bool(stat...  13.6 us
    ppermute x3, waiting for transfers between devices, on_device(): g = g + lax.ppermute(g, 'gx', [(a, a ^ step) for a in range(size_x)])  8.42 us
    ppermute x3, starting transfers between devices, on_device(): mine.append(lax.ppermute(slabs[k], 'gx', pairs))  6.03 us
    ppermute x3, waiting for transfers between devices, on_device(): mine.append(lax.ppermute(slabs[k], 'gx', pairs))  5.61 us
    ppermute x4, starting transfers between devices, on_device(): halo.append(lax.ppermute(slabs[k], 'gx', pairs))  3.9 us
    unnamed x10, local copies, waits for them, and re-layouts  3.85 us
    ppermute x3, starting transfers between devices, on_device(): g = g + lax.ppermute(g, 'gx', [(a, a ^ step) for a in range(size_x)])  3.46 us
  transfers between devices with their start and end apart: 15, of which 9 were waited for; matrix products, arithmetic and copies ran while one was open for 0% of the time, Pallas kernels for 15%

profile of v2, /device:TPU:0, one launch (start us, length us, event | category | flops | bytes accessed | tf_op | source)
XLA Modules:
  0.0 77.6 jit_solution(2921806830432284098)
XLA Ops:
  0.6 1.1 %copy-done = f32[4,2,4,5,4,256]{5,4,3,2,1,0:T(4,128)S(1)} copy-done((f32[4,2,4,5,4,256]{5,4,3,2,1,0:T(4,128)S(1)}, f32[4,2,4,5,4,256]{5,4,3,2,1,0:T(4,128)}, u32[]{:S(2)}) %copy-start) | copy-done | bytes 655384
  1.7 0.7 copy-done.1
  3.2 1.0 %pack.1 = (f32[48,8,128]{2,1,0:T(8,128)S(1)}, f32[48,8,128]{2,1,0:T(8,128)S(1)}, f32[48,8,128]{2,1,0:T(8,128)S(1)}, f32[48,8,128]{2,1,0:T(8,128)S(1)}) custom-call(f32[4,2,4,5,4,256]{5,4,3,2,1,0:T(4,128)S(1)} %copy-done, f32[4,4,256]{2,1,0:T(4,128)S(1)} %copy-done.1, f32[4,4,256]{2,1,0:T(4,128)S(1)} %copy-done.2), custom_call_target="tpu_custom_call" | custom-call | tf_op jit(solution)/shard_map/pack/pallas_call | solution.py:55
  4.1 3.0 %collective-permute-start.4 = (f32[48,8,128]{2,1,0:T(8,128)S(1)}, f32[48,8,128]{2,1,0:T(8,128)S(1)}, u32[]{:S(2)}, u32[]{:S(2)}) collective-permute-start(f32[48,8,128]{2,1,0:T(8,128)S(1)} %get-tuple-element.20), channel_id=1, source_target_pairs={{0,4},{4,8},{8,12},{12,0},{16,20},{20,24},{24,28},{28,16},{1,5},{5... | collective-permute-start | bytes 589832 | tf_op jit(solution)/shard_map/ppermute | solution.py:364
  7.1 1.6 %collective-permute-start.5 = (f32[48,8,128]{2,1,0:T(8,128)S(1)}, f32[48,8,128]{2,1,0:T(8,128)S(1)}, u32[]{:S(2)}, u32[]{:S(2)}) collective-permute-start(f32[48,8,128]{2,1,0:T(8,128)S(1)} %get-tuple-element.21), channel_id=1, source_target_pairs={{0,8},{4,12},{8,0},{12,4},{16,24},{20,28},{24,16},{28,20},{1,9},{5... | collective-permute-start | bytes 589832 | tf_op jit(solution)/shard_map/ppermute | solution.py:364
  8.7 1.4 %collective-permute-start.6 = (f32[48,8,128]{2,1,0:T(8,128)S(1)}, f32[48,8,128]{2,1,0:T(8,128)S(1)}, u32[]{:S(2)}, u32[]{:S(2)}) collective-permute-start(f32[48,8,128]{2,1,0:T(8,128)S(1)} %get-tuple-element.22), channel_id=1, source_target_pairs={{0,12},{4,0},{8,4},{12,8},{16,28},{20,16},{24,20},{28,24},{1,13},{... | collective-permute-start | bytes 589832 | tf_op jit(solution)/shard_map/ppermute | solution.py:364
  11.5 2.4 %collective-permute-done.4.refs_3_ = f32[48,8,128]{2,1,0:T(8,128)S(1)} collective-permute-done((f32[48,8,128]{2,1,0:T(8,128)S(1)}, f32[48,8,128]{2,1,0:T(8,128)S(1)}, u32[]{:S(2)}, u32[]{:S(2)}) %collective-permute-start.4) | collective-permute-done | bytes 196640 | tf_op jit(solution)/shard_map/ppermute | solution.py:364
  13.9 1.3 %collective-permute-start.3 = (f32[48,8,128]{2,1,0:T(8,128)S(1)}, f32[48,8,128]{2,1,0:T(8,128)S(1)}, u32[]{:S(2)}, u32[]{:S(2)}) collective-permute-start(f32[48,8,128]{2,1,0:T(8,128)S(1)} %get-tuple-element.22), channel_id=1, source_target_pairs={{8,20},{12,24},{16,12},{20,0},{9,21},{13,25},{17,13},{21,1},{10,22... | collective-permute-start | bytes 589832 | tf_op jit(solution)/shard_map/ppermute | solution.py:360
  15.2 3.2 %collective-permute-done.5.refs_4_ = f32[48,8,128]{2,1,0:T(8,128)S(1)} collective-permute-done((f32[48,8,128]{2,1,0:T(8,128)S(1)}, f32[48,8,128]{2,1,0:T(8,128)S(1)}, u32[]{:S(2)}, u32[]{:S(2)}) %collective-permute-start.5) | collective-permute-done | bytes 196640 | tf_op jit(solution)/shard_map/ppermute | solution.py:364
  18.4 1.3 %collective-permute-start = (f32[48,8,128]{2,1,0:T(8,128)S(1)}, f32[48,8,128]{2,1,0:T(8,128)S(1)}, u32[]{:S(2)}, u32[]{:S(2)}) collective-permute-start(f32[48,8,128]{2,1,0:T(8,128)S(1)} %get-tuple-element.19.refs_2_), channel_id=1, source_target_pairs={{8,24},{12,28},{16,0},{20,4},{9,25},{13,29},{17,1},{21,5},{10,26},... | collective-permute-start | bytes 589832 | tf_op jit(solution)/shard_map/ppermute | solution.py:360
  21.0 7.8 %inner.1 = (f32[16,10,8,128]{3,2,1,0:T(8,128)S(1)}, f32[260,8,128]{2,1,0:T(8,128)S(1)}, f32[260,8,128]{2,1,0:T(8,128)S(1)}, f32[260,8,128]{2,1,0:T(8,128)S(1)}, ...) custom-call(f32[5,5]{1,0:T(8,128)S(1)} %copy-done.3, ...), custom_call_target="tpu_custom_call" | custom-call | flops 6000000000 | bytes 1048576 | tf_op jit(solution)/shard_map/inner/pallas_call | solution.py:224
  28.9 2.6 %collective-permute-done.refs_2_ = f32[48,8,128]{2,1,0:T(8,128)S(1)} collective-permute-done((f32[48,8,128]{2,1,0:T(8,128)S(1)}, f32[48,8,128]{2,1,0:T(8,128)S(1)}, u32[]{:S(2)}, u32[]{:S(2)}) %collective-permute-start) | collective-permute-done | bytes 196640 | tf_op jit(solution)/shard_map/ppermute | solution.py:360
  31.5 5.8 %outer.1 = (f32[16,10,8,128]{3,2,1,0:T(8,128)S(1)}, f32[260,8,128]{2,1,0:T(8,128)S(1)}, f32[260,8,128]{2,1,0:T(8,128)S(1)}, f32[260,8,128]{2,1,0:T(8,128)S(1)}, ...) custom-call(f32[5,5]{1,0:T(8,128)S(1)} %copy-done.3, ...), custom_call_target="tpu_custom_call", output_to_operand_aliasing={{0}: (6, {}), {1}: (7, {}), {2}: (8, {}), {3}: (9, {}), {4}... | custom-call | flops 6000000000 | bytes 1048576 | tf_op jit(solution)/shard_map/outer/pallas_call | solution.py:224
  37.3 16.3 %all_to_all.5.y_ref.refs_0_ = f32[16,10,8,128]{3,2,1,0:T(8,128)S(1)} all-to-all(f32[16,10,8,128]{3,2,1,0:T(8,128)S(1)} %get-tuple-element.31), channel_id=1, replica_groups={{0,4,8,12,1,5,9,13,2,6,10,14,3,7,11,15},{16,20,24,28,17,21,25,29,18,22,..., dimensions={0} | all-to-all | bytes 1310720 | tf_op jit(solution)/shard_map/all_to_all | solution.py:371
  53.6 0.7 collective-permute-start.11
  54.4 1.8 %gram.1 = f32[16,16]{1,0:T(8,128)S(1)} custom-call(f32[16,10,8,128]{3,2,1,0:T(8,128)S(1)} %all_to_all.5.y_ref.refs_0_), custom_call_target="tpu_custom_call" | custom-call | flops 2000000000 | bytes 1048576 | tf_op jit(solution)/shard_map/gram/pallas_call | solution.py:262
  56.8 3.1 %collective-permute-done.7 = f32[16,16]{1,0:T(8,128)S(1)} collective-permute-done((f32[16,16]{1,0:T(8,128)S(1)}, f32[16,16]{1,0:T(8,128)S(1)}, u32[]{:S(2)}, u32[]{:S(2)}) %collective-permute-start.7) | collective-permute-done | bytes 1056 | tf_op jit(solution)/shard_map/ppermute | solution.py:378
  60.5 3.0 %collective-permute-done.8 = f32[16,16]{1,0:T(8,128)S(1)} collective-permute-done((f32[16,16]{1,0:T(8,128)S(1)}, f32[16,16]{1,0:T(8,128)S(1)}, u32[]{:S(2)}, u32[]{:S(2)}) %collective-permute-start.8) | collective-permute-done | bytes 1056 | tf_op jit(solution)/shard_map/ppermute | solution.py:378
  63.5 2.3 %collective-permute-start.9 = (f32[16,16]{1,0:T(8,128)S(1)}, f32[16,16]{1,0:T(8,128)S(1)}, u32[]{:S(2)}, u32[]{:S(2)}) collective-permute-start(f32[16,16]{1,0:T(8,128)S(1)} %add.16), channel_id=1, source_target_pairs={{0,16},{4,20},{8,24},{12,28},{16,0},{20,4},{24,8},{28,12},{1,17},{... | collective-permute-start | bytes 3080 | tf_op jit(solution)/shard_map/ppermute | solution.py:378
  65.8 2.3 %collective-permute-done.9 = f32[16,16]{1,0:T(8,128)S(1)} collective-permute-done((f32[16,16]{1,0:T(8,128)S(1)}, f32[16,16]{1,0:T(8,128)S(1)}, u32[]{:S(2)}, u32[]{:S(2)}) %collective-permute-start.9) | collective-permute-done | bytes 1056 | tf_op jit(solution)/shard_map/ppermute | solution.py:378
  69.3 1.1 %collective-permute-done.11.refs_2_ = f32[16,10,8,128]{3,2,1,0:T(8,128)S(1)} collective-permute-done((f32[16,10,8,128]{3,2,1,0:T(8,128)S(1)}, f32[16,10,8,128]{3,2,1,0:T(8,128)S(1)}, u32[]{:S(2)}, u32[]{:S(2)}) %collective-permute-start.11) | collective-permute-done | bytes 655392 | tf_op jit(solution)/shard_map/ppermute | solution.py:373
  70.9 3.1 %collective-permute-done.12 = f32[16,16]{1,0:T(8,128)S(1)} collective-permute-done((f32[16,16]{1,0:T(8,128)S(1)}, f32[16,16]{1,0:T(8,128)S(1)}, u32[]{:S(2)}, u32[]{:S(2)}) %collective-permute-start.12) | collective-permute-done | bytes 1056 | tf_op jit(solution)/shard_map/ppermute | solution.py:382
  74.0 1.9 %factor.1 = (f32[16,16]{1,0:T(8,128)}, f32[16,16]{1,0:T(8,128)S(1)}) custom-call(f32[16,16]{1,0:T(8,128)S(1)} %add.19.g_ref), custom_call_target="tpu_custom_call" | custom-call | tf_op jit(solution)/shard_map/factor/pallas_call | solution.py:294
  75.9 1.7 %basis.1 = f32[4,2,4,5,4,256]{5,4,3,2,1,0:T(4,128)} custom-call(f32[16,16]{1,0:T(8,128)S(1)} %get-tuple-element.33.linv_ref, f32[16,10,8,128]{3,2,1,0:T(8,128)S(1)} %all_to_all.5.y_ref.refs_0_, f32[16,10,8,128]{3,2,1,0:T(8,128)S(1)} %collective-permute-done.13.refs_1_, f32[16,10,8,128]{3,2,1,0:T(8,128)S(1)} %collective-permute-done.11.refs_2_, ...), custom_call_target="tpu_custom_call" | custom-call | tf_op jit(solution)/shard_map/basis/pallas_call | solution.py:331
  (28 shorter events, 6.3 us)
Async XLA Ops:
  0.6 1.1 %copy-start = (f32[4,2,4,5,4,256]{5,4,3,2,1,0:T(4,128)S(1)}, f32[4,2,4,5,4,256]{5,4,3,2,1,0:T(4,128)}, u32[]{:S(2)}) copy-start(f32[4,2,4,5,4,256]{5,4,3,2,1,0:T(4,128)} %forcing_hbm.1) | copy-start | bytes 1966084
  1.7 0.7 copy-start.1
  2.4 0.7 copy-start.2
  4.1 9.8 %collective-permute-start.4 = (f32[48,8,128]{2,1,0:T(8,128)S(1)}, f32[48,8,128]{2,1,0:T(8,128)S(1)}, u32[]{:S(2)}, u32[]{:S(2)}) collective-permute-start(f32[48,8,128]{2,1,0:T(8,128)S(1)} %get-tuple-element.20), channel_id=1, source_target_pairs={{0,4},{4,8},{8,12},{12,0},{16,20},{20,24},{24,28},{28,16},{1,5},{5... | collective-permute-start | bytes 589832 | tf_op jit(solution)/shard_map/ppermute | solution.py:364
  7.1 11.3 %collective-permute-start.5 = (f32[48,8,128]{2,1,0:T(8,128)S(1)}, f32[48,8,128]{2,1,0:T(8,128)S(1)}, u32[]{:S(2)}, u32[]{:S(2)}) collective-permute-start(f32[48,8,128]{2,1,0:T(8,128)S(1)} %get-tuple-element.21), channel_id=1, source_target_pairs={{0,8},{4,12},{8,0},{12,4},{16,24},{20,28},{24,16},{28,20},{1,9},{5... | collective-permute-start | bytes 589832 | tf_op jit(solution)/shard_map/ppermute | solution.py:364
  8.7 11.0 %collective-permute-start.6 = (f32[48,8,128]{2,1,0:T(8,128)S(1)}, f32[48,8,128]{2,1,0:T(8,128)S(1)}, u32[]{:S(2)}, u32[]{:S(2)}) collective-permute-start(f32[48,8,128]{2,1,0:T(8,128)S(1)} %get-tuple-element.22), channel_id=1, source_target_pairs={{0,12},{4,0},{8,4},{12,8},{16,28},{20,16},{24,20},{28,24},{1,13},{... | collective-permute-start | bytes 589832 | tf_op jit(solution)/shard_map/ppermute | solution.py:364
  10.2 21.3 %collective-permute-start.1 = (f32[48,8,128]{2,1,0:T(8,128)S(1)}, f32[48,8,128]{2,1,0:T(8,128)S(1)}, u32[]{:S(2)}, u32[]{:S(2)}) collective-permute-start(f32[48,8,128]{2,1,0:T(8,128)S(1)} %get-tuple-element.20), channel_id=1, source_target_pairs={{8,28},{12,16},{16,4},{20,8},{9,29},{13,17},{17,5},{21,9},{10,30},... | collective-permute-start | bytes 589832 | tf_op jit(solution)/shard_map/ppermute | solution.py:360
  10.8 20.6 %collective-permute-start.2 = (f32[48,8,128]{2,1,0:T(8,128)S(1)}, f32[48,8,128]{2,1,0:T(8,128)S(1)}, u32[]{:S(2)}, u32[]{:S(2)}) collective-permute-start(f32[48,8,128]{2,1,0:T(8,128)S(1)} %get-tuple-element.21), channel_id=1, source_target_pairs={{8,16},{12,20},{16,8},{20,12},{9,17},{13,21},{17,9},{21,13},{10,18... | collective-permute-start | bytes 589832 | tf_op jit(solution)/shard_map/ppermute | solution.py:360
  13.9 17.5 %collective-permute-start.3 = (f32[48,8,128]{2,1,0:T(8,128)S(1)}, f32[48,8,128]{2,1,0:T(8,128)S(1)}, u32[]{:S(2)}, u32[]{:S(2)}) collective-permute-start(f32[48,8,128]{2,1,0:T(8,128)S(1)} %get-tuple-element.22), channel_id=1, source_target_pairs={{8,20},{12,24},{16,12},{20,0},{9,21},{13,25},{17,13},{21,1},{10,22... | collective-permute-start | bytes 589832 | tf_op jit(solution)/shard_map/ppermute | solution.py:360
  18.4 13.1 %collective-permute-start = (f32[48,8,128]{2,1,0:T(8,128)S(1)}, f32[48,8,128]{2,1,0:T(8,128)S(1)}, u32[]{:S(2)}, u32[]{:S(2)}) collective-permute-start(f32[48,8,128]{2,1,0:T(8,128)S(1)} %get-tuple-element.19.refs_2_), channel_id=1, source_target_pairs={{8,24},{12,28},{16,0},{20,4},{9,25},{13,29},{17,1},{21,5},{10,26},... | collective-permute-start | bytes 589832 | tf_op jit(solution)/shard_map/ppermute | solution.py:360
  19.7 0.7 copy-start.3
  20.4 0.7 copy-start.4
  53.6 16.8 %collective-permute-start.11 = (f32[16,10,8,128]{3,2,1,0:T(8,128)S(1)}, f32[16,10,8,128]{3,2,1,0:T(8,128)S(1)}, u32[]{:S(2)}, u32[]{:S(2)}) collective-permute-start(f32[16,10,8,128]{3,2,1,0:T(8,128)S(1)} %all_to_all.5.y_ref.refs_0_), channel_id=1, source_target_pairs={{0,2},{1,3},{2,0},{3,1},{4,6},{5,7},{6,4},{7,5},{8,10},{9,11},{10,... | collective-permute-start | bytes 1966088 | tf_op jit(solution)/shard_map/ppermute | solution.py:373
  56.2 3.7 %collective-permute-start.7 = (f32[16,16]{1,0:T(8,128)S(1)}, f32[16,16]{1,0:T(8,128)S(1)}, u32[]{:S(2)}, u32[]{:S(2)}) collective-permute-start(f32[16,16]{1,0:T(8,128)S(1)} %gram.1), channel_id=1, source_target_pairs={{0,4},{4,0},{8,12},{12,8},{16,20},{20,16},{24,28},{28,24},{1,5},{5... | collective-permute-start | bytes 3080 | tf_op jit(solution)/shard_map/ppermute | solution.py:378
  59.9 3.7 %collective-permute-start.8 = (f32[16,16]{1,0:T(8,128)S(1)}, f32[16,16]{1,0:T(8,128)S(1)}, u32[]{:S(2)}, u32[]{:S(2)}) collective-permute-start(f32[16,16]{1,0:T(8,128)S(1)} %add.15), channel_id=1, source_target_pairs={{0,8},{4,12},{8,0},{12,4},{16,24},{20,28},{24,16},{28,20},{1,9},{5... | collective-permute-start | bytes 3080 | tf_op jit(solution)/shard_map/ppermute | solution.py:378
  63.5 4.6 %collective-permute-start.9 = (f32[16,16]{1,0:T(8,128)S(1)}, f32[16,16]{1,0:T(8,128)S(1)}, u32[]{:S(2)}, u32[]{:S(2)}) collective-permute-start(f32[16,16]{1,0:T(8,128)S(1)} %add.16), channel_id=1, source_target_pairs={{0,16},{4,20},{8,24},{12,28},{16,0},{20,4},{24,8},{28,12},{1,17},{... | collective-permute-start | bytes 3080 | tf_op jit(solution)/shard_map/ppermute | solution.py:378
  68.1 1.2 %collective-permute-start.10 = (f32[16,16]{1,0:T(8,128)S(1)}, f32[16,16]{1,0:T(8,128)S(1)}, u32[]{:S(2)}, u32[]{:S(2)}) collective-permute-start(f32[16,16]{1,0:T(8,128)S(1)} %add.17), channel_id=1, source_target_pairs={{0,1},{1,0},{2,3},{3,2},{4,5},{5,4},{6,7},{7,6},{8,9},{9,8},{10,11... | collective-permute-start | bytes 3080 | tf_op jit(solution)/shard_map/ppermute | solution.py:380
  68.1 7.8 %collective-permute-start.13 = (f32[16,10,8,128]{3,2,1,0:T(8,128)S(1)}, f32[16,10,8,128]{3,2,1,0:T(8,128)S(1)}, u32[]{:S(2)}, u32[]{:S(2)}) collective-permute-start(f32[16,10,8,128]{3,2,1,0:T(8,128)S(1)} %all_to_all.5.y_ref.refs_0_), channel_id=1, source_target_pairs={{0,1},{1,0},{2,3},{3,2},{4,5},{5,4},{6,7},{7,6},{8,9},{9,8},{10,11... | collective-permute-start | bytes 1966088 | tf_op jit(solution)/shard_map/ppermute | solution.py:374
  70.4 5.5 %collective-permute-start.14 = (f32[16,10,8,128]{3,2,1,0:T(8,128)S(1)}, f32[16,10,8,128]{3,2,1,0:T(8,128)S(1)}, u32[]{:S(2)}, u32[]{:S(2)}) collective-permute-start(f32[16,10,8,128]{3,2,1,0:T(8,128)S(1)} %collective-permute-done.11.refs_2_), channel_id=1, source_target_pairs={{0,1},{1,0},{2,3},{3,2},{4,5},{5,4},{6,7},{7,6},{8,9},{9,8},{10,11... | collective-permute-start | bytes 1966088 | tf_op jit(solution)/shard_map/ppermute | solution.py:383
  70.4 3.7 %collective-permute-start.12 = (f32[16,16]{1,0:T(8,128)S(1)}, f32[16,16]{1,0:T(8,128)S(1)}, u32[]{:S(2)}, u32[]{:S(2)}) collective-permute-start(f32[16,16]{1,0:T(8,128)S(1)} %add.18), channel_id=1, source_target_pairs={{0,2},{1,3},{2,0},{3,1},{4,6},{5,7},{6,4},{7,5},{8,10},{9,11},{10,... | collective-permute-start | bytes 3080 | tf_op jit(solution)/shard_map/ppermute | solution.py:382

commit v3 on v2

--- a/solution.py
+++ b/solution.py
@@ -6,6 +6,7 @@
 from jax.experimental import pallas as pl
 from jax.experimental.pallas import tpu as pltpu
 from jax.sharding import PartitionSpec as P
+
 
 FORCINGS = 8
 SWEEPS = 8
@@ -26,7 +27,7 @@
     rows = parts * planes * nvar
     copies = []
     for k in range(cols):
-        col = lax.rem(me + k, cols)
+        col = lax.bitwise_xor(me, k)
         copies.append(pltpu.make_async_copy(forcing_hbm.at[col], forcing_ref.at[k], sems.at[k]))
     copies.append(pltpu.make_async_copy(sponge_hbm, sponge_ref, sems.at[cols]))
     copies.append(pltpu.make_async_copy(flow_hbm, flow_ref, sems.at[cols + 1]))
@@ -48,6 +49,10 @@
                     out_ref[row] = fold(forcing_ref[k, part, plane, v])
 
 
+def in_place(*arrays):
+    return tuple(pltpu.with_memory_space_constraint(a, pltpu.HBM) for a in arrays)
+
+
 def pack(forcing, sponge, flow):
     cols, parts, planes, nvar = forcing.shape[:4]
     rows = planes * (parts * nvar + 2)
@@ -65,7 +70,7 @@
         ],
         compiler_params=pltpu.CompilerParams(vmem_limit_bytes=4 << 20),
         name="pack",
-    )(forcing, sponge, flow)
+    )(*in_place(forcing, sponge, flow))
 
 
 def sweep_kernel(dims, two_sided, outer, *refs):
@@ -94,7 +99,7 @@
         copy.start()
     copies = []
     for k, slab_ref in enumerate(slab_refs):
-        slot = lax.rem(me + cols - k, cols)
+        slot = lax.bitwise_xor(me, k)
         copies.append(pltpu.make_async_copy(slab_ref, raw.at[pl.ds(slot * rows, rows)], sems.at[k]))
         copies[-1].start()
 
@@ -212,7 +217,7 @@
 
 
 def sweeps(coupling, omega, slabs, dims, two_sided, state=()):
-    cols, parts, planes, nvar, groups = dims
+    cols, parts, planes, nvar, _ = dims
     comp = parts * nvar
     own = cols * planes
     window = own + SWEEPS * (2 if two_sided else 1)
@@ -238,7 +243,7 @@
         compiler_params=pltpu.CompilerParams(vmem_limit_bytes=16 << 20),
         cost_estimate=pl.CostEstimate(flops=6_000_000_000, bytes_accessed=1 << 20, transcendentals=0),
         name="outer" if state else "inner",
-    )(coupling, omega, *slabs, *state)
+    )(*in_place(coupling, omega), *slabs, *state)
 
 
 def gram_kernel(y_ref, g_ref):
@@ -303,7 +308,7 @@
 
 def basis_kernel(linv_ref, *refs):
     y_refs, out_ref, table = refs[:-2], refs[-2], refs[-1]
-    cols, parts, planes, nvar = out_ref.shape[:4]
+    cols, parts, _, nvar = out_ref.shape[:4]
     count = linv_ref.shape[0]
     af = lax.axis_index("af")
     for c in range(cols):
@@ -343,7 +348,6 @@
     cols, parts, planes, nvar, rad, azi = forcing.shape
     groups = size_x // cols
     two_sided = groups != 2
-    count = cols * size_f
     assert rad * azi == SUB * LANE and azi == 2 * LANE and size_x % cols == 0
     assert planes == size_f and 2 * planes == SWEEPS and cols == 4
     dims = (cols, parts, planes, nvar, groups)
@@ -356,11 +360,11 @@
             group, j = divmod(g, cols)
             target = group - 1 if j < cols // 2 else group + 1
             if 0 <= target < groups:
-                pairs.append((g, target * cols + (j + k) % cols))
+                pairs.append((g, target * cols + (j ^ k)))
         halo.append(lax.ppermute(slabs[k], "gx", pairs))
     mine = [slabs[0]]
     for k in range(1, cols):
-        pairs = [(g, g // cols * cols + (g + k) % cols) for g in range(size_x)]
+        pairs = [(g, g ^ k) for g in range(size_x)]
         mine.append(lax.ppermute(slabs[k], "gx", pairs))
     state = sweeps(coupling, omega, mine, dims, two_sided)
     z = sweeps(coupling, omega, halo, dims, two_sided, state)[0]
@@ -375,12 +379,17 @@
     g = gram(y)
     step = 1
     while step < size_x:
-        g = g + lax.ppermute(g, "gx", [(a, a ^ step) for a in range(size_x)])
-        step *= 2
-    g = g + lax.ppermute(g, "af", [(a, a ^ 1) for a in range(size_f)])
+        far = min(4, size_x // step) if step > 1 else 2
+        others = [
+            lax.ppermute(g, "gx", [(x, x ^ (step * k)) for x in range(size_x)]) for k in range(1, far)
+        ]
+        for other in others:
+            g = g + other
+        step *= far
+    for k in (1, 2):
+        g = g + lax.ppermute(g, "af", [(x, x ^ k) for x in range(size_f)])
     g, ys[2] = lax.optimization_barrier((g, ys[2]))
-    g = g + lax.ppermute(g, "af", [(a, a ^ 2) for a in range(size_f)])
-    ys[3] = lax.ppermute(ys[2], "af", [(a, a ^ 1) for a in range(size_f)])
+    ys[3] = lax.ppermute(ys[2], "af", [(x, x ^ 1) for x in range(size_f)])
     length = parts * planes * nvar * rad * azi * size_x
     coeff, linv = factor(g, length)
     return basis_of(linv, ys, forcing.shape), coeff
@@ -394,8 +403,12 @@
         P(),
         P(),
     )
+
+    def body(*args):
+        return on_device(mesh.shape["gx"], mesh.shape["af"], *args)
+
     return jax.shard_map(
-        functools.partial(on_device, mesh.shape["gx"], mesh.shape["af"]),
+        body,
         mesh=mesh,
         in_specs=placed,
         out_specs=(P("af", None, "gx", None, None, None), P()),

time: 78 us -> 72.7 us (0.932)
  local copies, waits for them, and re-layouts: 3.85 us -> 0 us
  blocking collectives: 16.3 us -> 14.5 us
    unnamed x10 -> x0, local copies, waits for them, and re-layouts: 3.85 us -> none
    ppermute x3, waiting for transfers between devices: 5.61 us -> 9.08 us  [on_device(): mine.append(lax.ppermute(slabs[k], 'gx', pairs))]
    ppermute x6 -> x7, starting transfers between devices: 4.03 us -> 6.33 us  [the longest x4 4.97 us: on_device(): lax.ppermute(g, 'gx', [(x, x ^ step * k) for x in range(size_x)])]
    all_to_all x1, blocking collectives: 16.3 us -> 14.5 us  [on_device(): lax.all_to_all(z, ('gx', 'af'), 0, 0, axis_index_groups=together, tiled=T...]
    ppermute x6 -> x7, waiting for transfers between devices: 12.2 us -> 10.5 us  [the longest x4 6.71 us: on_device(): lax.ppermute(g, 'gx', [(x, x ^ step * k) for x in range(size_x)])]
    ppermute x3, starting transfers between devices: 6.03 us -> 4.61 us  [on_device(): mine.append(lax.ppermute(slabs[k], 'gx', pairs))]
    ppermute x1, waiting for transfers between devices: 1.1 us -> 0.01 us  [on_device(): ys[2] = lax.ppermute(y, 'af', [(a, a ^ 2) for a in range(size_f)])]
  transfers between devices with their start and end apart: 15 -> 16, of which waited for: 9 -> 10; matrix products, arithmetic and copies ran while one was open for 0% -> 0% of each run, Pallas kernels for 15% -> 16%
where the time goes in v3:
time: 72.7 us; the launch traced here: 72.4 us
  waiting for transfers between devices  21.7 us (30%)
  Pallas kernels  19.8 us (27%)
  starting transfers between devices  15.6 us (21%)
  blocking collectives  14.5 us (20%)
    all_to_all x1, blocking collectives, on_device(): lax.all_to_all(z, ('gx', 'af'), 0, 0, axis_index_groups=together, tiled=T...  14.5 us
    pallas_call x2, Pallas kernels, sweeps(): pl.pallas_call(functools.partial(sweep_kernel, dims, two_sided, bool(stat...  13.2 us
    ppermute x3, waiting for transfers between devices, on_device(): mine.append(lax.ppermute(slabs[k], 'gx', pairs))  9.08 us
    ppermute x4, waiting for transfers between devices, on_device(): lax.ppermute(g, 'gx', [(x, x ^ step * k) for x in range(size_x)])  6.71 us
    ppermute x4, starting transfers between devices, on_device(): lax.ppermute(g, 'gx', [(x, x ^ step * k) for x in range(size_x)])  4.97 us
    ppermute x3, starting transfers between devices, on_device(): mine.append(lax.ppermute(slabs[k], 'gx', pairs))  4.61 us
    ppermute x4, starting transfers between devices, on_device(): halo.append(lax.ppermute(slabs[k], 'gx', pairs))  3.9 us
    ppermute x2, waiting for transfers between devices, on_device(): g = g + lax.ppermute(g, 'af', [(x, x ^ k) for x in range(size_f)])  3.52 us
  transfers between devices with their start and end apart: 16, of which 10 were waited for; matrix products, arithmetic and copies ran while one was open for 0% of the time, Pallas kernels for 16%

profile of v3, /device:TPU:0, one launch (start us, length us, event | category | flops | bytes accessed | tf_op | source)
XLA Modules:
  0.0 72.4 jit_solution(8268380358777312016)
XLA Ops:
  0.6 1.2 %pack.1 = (f32[48,8,128]{2,1,0:T(8,128)S(1)}, f32[48,8,128]{2,1,0:T(8,128)S(1)}, f32[48,8,128]{2,1,0:T(8,128)S(1)}, f32[48,8,128]{2,1,0:T(8,128)S(1)}) custom-call(f32[4,2,4,5,4,256]{5,4,3,2,1,0:T(4,128)} %forcing_hbm.1, f32[4,4,256]{2,1,0:T(4,128)} %sponge_hbm.1, f32[4,4,256]{2,1,0:T(4,128)} %flow_hbm.1), custom_call_target="tpu_custom_call" | custom-call | tf_op jit(solution)/shard_map/pack/pallas_call | solution.py:60
  1.9 3.0 %collective-permute-start.4 = (f32[48,8,128]{2,1,0:T(8,128)S(1)}, f32[48,8,128]{2,1,0:T(8,128)S(1)}, u32[]{:S(2)}, u32[]{:S(2)}) collective-permute-start(f32[48,8,128]{2,1,0:T(8,128)S(1)} %get-tuple-element.20), channel_id=1, source_target_pairs={{0,4},{4,0},{8,12},{12,8},{16,20},{20,16},{24,28},{28,24},{1,5},{5... | collective-permute-start | bytes 589832 | tf_op jit(solution)/shard_map/ppermute | solution.py:368
  4.9 1.6 %collective-permute-start.5 = (f32[48,8,128]{2,1,0:T(8,128)S(1)}, f32[48,8,128]{2,1,0:T(8,128)S(1)}, u32[]{:S(2)}, u32[]{:S(2)}) collective-permute-start(f32[48,8,128]{2,1,0:T(8,128)S(1)} %get-tuple-element.21), channel_id=1, source_target_pairs={{0,8},{4,12},{8,0},{12,4},{16,24},{20,28},{24,16},{28,20},{1,9},{5... | collective-permute-start | bytes 589832 | tf_op jit(solution)/shard_map/ppermute | solution.py:368
  6.5 1.3 %collective-permute-start.1 = (f32[48,8,128]{2,1,0:T(8,128)S(1)}, f32[48,8,128]{2,1,0:T(8,128)S(1)}, u32[]{:S(2)}, u32[]{:S(2)}) collective-permute-start(f32[48,8,128]{2,1,0:T(8,128)S(1)} %get-tuple-element.20), channel_id=1, source_target_pairs={{8,28},{12,24},{16,4},{20,0},{9,29},{13,25},{17,5},{21,1},{10,30},... | collective-permute-start | bytes 589832 | tf_op jit(solution)/shard_map/ppermute | solution.py:364
  8.4 1.4 %collective-permute-done.4.refs_3_ = f32[48,8,128]{2,1,0:T(8,128)S(1)} collective-permute-done((f32[48,8,128]{2,1,0:T(8,128)S(1)}, f32[48,8,128]{2,1,0:T(8,128)S(1)}, u32[]{:S(2)}, u32[]{:S(2)}) %collective-permute-start.4) | collective-permute-done | bytes 196640 | tf_op jit(solution)/shard_map/ppermute | solution.py:368
  10.5 6.4 %collective-permute-done.5.refs_4_ = f32[48,8,128]{2,1,0:T(8,128)S(1)} collective-permute-done((f32[48,8,128]{2,1,0:T(8,128)S(1)}, f32[48,8,128]{2,1,0:T(8,128)S(1)}, u32[]{:S(2)}, u32[]{:S(2)}) %collective-permute-start.5) | collective-permute-done | bytes 196640 | tf_op jit(solution)/shard_map/ppermute | solution.py:368
  16.9 1.3 %collective-permute-start = (f32[48,8,128]{2,1,0:T(8,128)S(1)}, f32[48,8,128]{2,1,0:T(8,128)S(1)}, u32[]{:S(2)}, u32[]{:S(2)}) collective-permute-start(f32[48,8,128]{2,1,0:T(8,128)S(1)} %get-tuple-element.19.refs_2_), channel_id=1, source_target_pairs={{8,24},{12,28},{16,0},{20,4},{9,25},{13,29},{17,1},{21,5},{10,26},... | collective-permute-start | bytes 589832 | tf_op jit(solution)/shard_map/ppermute | solution.py:364
  18.2 1.3 %collective-permute-done.6.refs_5_ = f32[48,8,128]{2,1,0:T(8,128)S(1)} collective-permute-done((f32[48,8,128]{2,1,0:T(8,128)S(1)}, f32[48,8,128]{2,1,0:T(8,128)S(1)}, u32[]{:S(2)}, u32[]{:S(2)}) %collective-permute-start.6) | collective-permute-done | bytes 196640 | tf_op jit(solution)/shard_map/ppermute | solution.py:368
  19.5 7.6 %inner.1 = (f32[16,10,8,128]{3,2,1,0:T(8,128)S(1)}, f32[260,8,128]{2,1,0:T(8,128)S(1)}, f32[260,8,128]{2,1,0:T(8,128)S(1)}, f32[260,8,128]{2,1,0:T(8,128)S(1)}, ...) custom-call(f32[5,5]{1,0:T(8,128)} %refs_0_.3, ...), custom_call_target="tpu_custom_call" | custom-call | flops 6000000000 | bytes 1048576 | tf_op jit(solution)/shard_map/inner/pallas_call | solution.py:229
  27.1 2.1 %collective-permute-done.refs_2_ = f32[48,8,128]{2,1,0:T(8,128)S(1)} collective-permute-done((f32[48,8,128]{2,1,0:T(8,128)S(1)}, f32[48,8,128]{2,1,0:T(8,128)S(1)}, u32[]{:S(2)}, u32[]{:S(2)}) %collective-permute-start) | collective-permute-done | bytes 196640 | tf_op jit(solution)/shard_map/ppermute | solution.py:364
  29.2 5.7 %outer.1 = (f32[16,10,8,128]{3,2,1,0:T(8,128)S(1)}, f32[260,8,128]{2,1,0:T(8,128)S(1)}, f32[260,8,128]{2,1,0:T(8,128)S(1)}, f32[260,8,128]{2,1,0:T(8,128)S(1)}, ...) custom-call(f32[5,5]{1,0:T(8,128)} %refs_0_.3, ...), custom_call_target="tpu_custom_call", output_to_operand_aliasing={{0}: (6, {}), {1}: (7, {}), {2}: (8, {}), {3}: (9, {}), {4}... | custom-call | flops 6000000000 | bytes 1048576 | tf_op jit(solution)/shard_map/outer/pallas_call | solution.py:229
  34.9 14.5 %all_to_all.5.y_ref.refs_0_ = f32[16,10,8,128]{3,2,1,0:T(8,128)S(1)} all-to-all(f32[16,10,8,128]{3,2,1,0:T(8,128)S(1)} %get-tuple-element.31), channel_id=1, replica_groups={{0,4,8,12,1,5,9,13,2,6,10,14,3,7,11,15},{16,20,24,28,17,21,25,29,18,22,..., dimensions={0} | all-to-all | bytes 1310720 | tf_op jit(solution)/shard_map/all_to_all | solution.py:375
  49.4 0.7 %collective-permute-start.13 = (f32[16,10,8,128]{3,2,1,0:T(8,128)S(1)}, f32[16,10,8,128]{3,2,1,0:T(8,128)S(1)}, u32[]{:S(2)}, u32[]{:S(2)}) collective-permute-start(f32[16,10,8,128]{3,2,1,0:T(8,128)S(1)} %all_to_all.5.y_ref.refs_0_), channel_id=1, source_target_pairs={{0,2},{1,3},{2,0},{3,1},{4,6},{5,7},{6,4},{7,5},{8,10},{9,11},{10,... | collective-permute-start | bytes 1966088 | tf_op jit(solution)/shard_map/ppermute | solution.py:377
  50.1 1.8 %gram.1 = f32[16,16]{1,0:T(8,128)S(1)} custom-call(f32[16,10,8,128]{3,2,1,0:T(8,128)S(1)} %all_to_all.5.y_ref.refs_0_), custom_call_target="tpu_custom_call" | custom-call | flops 2000000000 | bytes 1048576 | tf_op jit(solution)/shard_map/gram/pallas_call | solution.py:267
  52.6 3.1 %collective-permute-done.7 = f32[16,16]{1,0:T(8,128)S(1)} collective-permute-done((f32[16,16]{1,0:T(8,128)S(1)}, f32[16,16]{1,0:T(8,128)S(1)}, u32[]{:S(2)}, u32[]{:S(2)}) %collective-permute-start.7) | collective-permute-done | bytes 1056 | tf_op jit(solution)/shard_map/ppermute | solution.py:384
  55.7 3.4 %collective-permute-start.10 = (f32[16,16]{1,0:T(8,128)S(1)}, f32[16,16]{1,0:T(8,128)S(1)}, u32[]{:S(2)}, u32[]{:S(2)}) collective-permute-start(f32[16,16]{1,0:T(8,128)S(1)} %add.18), channel_id=1, source_target_pairs={{0,24},{4,28},{8,16},{12,20},{16,8},{20,12},{24,0},{28,4},{1,25},{... | collective-permute-start | bytes 3080 | tf_op jit(solution)/shard_map/ppermute | solution.py:384
  59.1 1.0 %collective-permute-start.8 = (f32[16,16]{1,0:T(8,128)S(1)}, f32[16,16]{1,0:T(8,128)S(1)}, u32[]{:S(2)}, u32[]{:S(2)}) collective-permute-start(f32[16,16]{1,0:T(8,128)S(1)} %add.18), channel_id=1, source_target_pairs={{0,8},{4,12},{8,0},{12,4},{16,24},{20,28},{24,16},{28,20},{1,9},{5... | collective-permute-start | bytes 3080 | tf_op jit(solution)/shard_map/ppermute | solution.py:384
  60.0 1.1 %collective-permute-done.10 = f32[16,16]{1,0:T(8,128)S(1)} collective-permute-done((f32[16,16]{1,0:T(8,128)S(1)}, f32[16,16]{1,0:T(8,128)S(1)}, u32[]{:S(2)}, u32[]{:S(2)}) %collective-permute-start.10) | collective-permute-done | bytes 1056 | tf_op jit(solution)/shard_map/ppermute | solution.py:384
  61.2 2.5 %collective-permute-done.9 = f32[16,16]{1,0:T(8,128)S(1)} collective-permute-done((f32[16,16]{1,0:T(8,128)S(1)}, f32[16,16]{1,0:T(8,128)S(1)}, u32[]{:S(2)}, u32[]{:S(2)}) %collective-permute-start.9) | collective-permute-done | bytes 1056 | tf_op jit(solution)/shard_map/ppermute | solution.py:384
  63.8 1.2 %collective-permute-done.11 = f32[16,16]{1,0:T(8,128)S(1)} collective-permute-done((f32[16,16]{1,0:T(8,128)S(1)}, f32[16,16]{1,0:T(8,128)S(1)}, u32[]{:S(2)}, u32[]{:S(2)}) %collective-permute-start.11) | collective-permute-done | bytes 1056 | tf_op jit(solution)/shard_map/ppermute | solution.py:390
  64.9 1.3 %collective-permute-start.12 = (f32[16,16]{1,0:T(8,128)S(1)}, f32[16,16]{1,0:T(8,128)S(1)}, u32[]{:S(2)}, u32[]{:S(2)}) collective-permute-start(f32[16,16]{1,0:T(8,128)S(1)} %add.22), channel_id=1, source_target_pairs={{0,2},{1,3},{2,0},{3,1},{4,6},{5,7},{6,4},{7,5},{8,10},{9,11},{10,... | collective-permute-start | bytes 3080 | tf_op jit(solution)/shard_map/ppermute | solution.py:390
  66.2 2.4 %collective-permute-done.12 = f32[16,16]{1,0:T(8,128)S(1)} collective-permute-done((f32[16,16]{1,0:T(8,128)S(1)}, f32[16,16]{1,0:T(8,128)S(1)}, u32[]{:S(2)}, u32[]{:S(2)}) %collective-permute-start.12) | collective-permute-done | bytes 1056 | tf_op jit(solution)/shard_map/ppermute | solution.py:390
  68.6 1.9 %factor.1 = (f32[16,16]{1,0:T(8,128)}, f32[16,16]{1,0:T(8,128)S(1)}) custom-call(f32[16,16]{1,0:T(8,128)S(1)} %add.23.g_ref), custom_call_target="tpu_custom_call" | custom-call | tf_op jit(solution)/shard_map/factor/pallas_call | solution.py:299
  70.7 1.7 %basis.1 = f32[4,2,4,5,4,256]{5,4,3,2,1,0:T(4,128)} custom-call(f32[16,16]{1,0:T(8,128)S(1)} %get-tuple-element.33.linv_ref, f32[16,10,8,128]{3,2,1,0:T(8,128)S(1)} %all_to_all.5.y_ref.refs_0_, f32[16,10,8,128]{3,2,1,0:T(8,128)S(1)} %collective-permute-done.14.refs_1_, f32[16,10,8,128]{3,2,1,0:T(8,128)S(1)} %collective-permute-done.13.refs_2_, ...), custom_call_target="tpu_custom_call" | custom-call | tf_op jit(solution)/shard_map/basis/pallas_call | solution.py:336
  (19 shorter events, 2.3 us)
Async XLA Ops:
  1.9 7.9 %collective-permute-start.4 = (f32[48,8,128]{2,1,0:T(8,128)S(1)}, f32[48,8,128]{2,1,0:T(8,128)S(1)}, u32[]{:S(2)}, u32[]{:S(2)}) collective-permute-start(f32[48,8,128]{2,1,0:T(8,128)S(1)} %get-tuple-element.20), channel_id=1, source_target_pairs={{0,4},{4,0},{8,12},{12,8},{16,20},{20,16},{24,28},{28,24},{1,5},{5... | collective-permute-start | bytes 589832 | tf_op jit(solution)/shard_map/ppermute | solution.py:368
  4.9 12.0 %collective-permute-start.5 = (f32[48,8,128]{2,1,0:T(8,128)S(1)}, f32[48,8,128]{2,1,0:T(8,128)S(1)}, u32[]{:S(2)}, u32[]{:S(2)}) collective-permute-start(f32[48,8,128]{2,1,0:T(8,128)S(1)} %get-tuple-element.21), channel_id=1, source_target_pairs={{0,8},{4,12},{8,0},{12,4},{16,24},{20,28},{24,16},{28,20},{1,9},{5... | collective-permute-start | bytes 589832 | tf_op jit(solution)/shard_map/ppermute | solution.py:368
  6.5 13.0 %collective-permute-start.6 = (f32[48,8,128]{2,1,0:T(8,128)S(1)}, f32[48,8,128]{2,1,0:T(8,128)S(1)}, u32[]{:S(2)}, u32[]{:S(2)}) collective-permute-start(f32[48,8,128]{2,1,0:T(8,128)S(1)} %get-tuple-element.22), channel_id=1, source_target_pairs={{0,12},{4,8},{8,4},{12,0},{16,28},{20,24},{24,20},{28,16},{1,13},{... | collective-permute-start | bytes 589832 | tf_op jit(solution)/shard_map/ppermute | solution.py:368
  6.5 22.7 %collective-permute-start.1 = (f32[48,8,128]{2,1,0:T(8,128)S(1)}, f32[48,8,128]{2,1,0:T(8,128)S(1)}, u32[]{:S(2)}, u32[]{:S(2)}) collective-permute-start(f32[48,8,128]{2,1,0:T(8,128)S(1)} %get-tuple-element.20), channel_id=1, source_target_pairs={{8,28},{12,24},{16,4},{20,0},{9,29},{13,25},{17,5},{21,1},{10,30},... | collective-permute-start | bytes 589832 | tf_op jit(solution)/shard_map/ppermute | solution.py:364
  7.8 21.4 %collective-permute-start.2 = (f32[48,8,128]{2,1,0:T(8,128)S(1)}, f32[48,8,128]{2,1,0:T(8,128)S(1)}, u32[]{:S(2)}, u32[]{:S(2)}) collective-permute-start(f32[48,8,128]{2,1,0:T(8,128)S(1)} %get-tuple-element.21), channel_id=1, source_target_pairs={{8,16},{12,20},{16,8},{20,12},{9,17},{13,21},{17,9},{21,13},{10,18... | collective-permute-start | bytes 589832 | tf_op jit(solution)/shard_map/ppermute | solution.py:364
  9.8 19.4 %collective-permute-start.3 = (f32[48,8,128]{2,1,0:T(8,128)S(1)}, f32[48,8,128]{2,1,0:T(8,128)S(1)}, u32[]{:S(2)}, u32[]{:S(2)}) collective-permute-start(f32[48,8,128]{2,1,0:T(8,128)S(1)} %get-tuple-element.22), channel_id=1, source_target_pairs={{8,20},{12,16},{16,12},{20,8},{9,21},{13,17},{17,13},{21,9},{10,22... | collective-permute-start | bytes 589832 | tf_op jit(solution)/shard_map/ppermute | solution.py:364
  16.9 12.3 %collective-permute-start = (f32[48,8,128]{2,1,0:T(8,128)S(1)}, f32[48,8,128]{2,1,0:T(8,128)S(1)}, u32[]{:S(2)}, u32[]{:S(2)}) collective-permute-start(f32[48,8,128]{2,1,0:T(8,128)S(1)} %get-tuple-element.19.refs_2_), channel_id=1, source_target_pairs={{8,24},{12,28},{16,0},{20,4},{9,25},{13,29},{17,1},{21,5},{10,26},... | collective-permute-start | bytes 589832 | tf_op jit(solution)/shard_map/ppermute | solution.py:364
  49.4 19.2 %collective-permute-start.13 = (f32[16,10,8,128]{3,2,1,0:T(8,128)S(1)}, f32[16,10,8,128]{3,2,1,0:T(8,128)S(1)}, u32[]{:S(2)}, u32[]{:S(2)}) collective-permute-start(f32[16,10,8,128]{3,2,1,0:T(8,128)S(1)} %all_to_all.5.y_ref.refs_0_), channel_id=1, source_target_pairs={{0,2},{1,3},{2,0},{3,1},{4,6},{5,7},{6,4},{7,5},{8,10},{9,11},{10,... | collective-permute-start | bytes 1966088 | tf_op jit(solution)/shard_map/ppermute | solution.py:377
  52.0 3.7 %collective-permute-start.7 = (f32[16,16]{1,0:T(8,128)S(1)}, f32[16,16]{1,0:T(8,128)S(1)}, u32[]{:S(2)}, u32[]{:S(2)}) collective-permute-start(f32[16,16]{1,0:T(8,128)S(1)} %gram.1), channel_id=1, source_target_pairs={{0,4},{4,0},{8,12},{12,8},{16,20},{20,16},{24,28},{28,24},{1,5},{5... | collective-permute-start | bytes 3080 | tf_op jit(solution)/shard_map/ppermute | solution.py:384
  55.7 5.5 %collective-permute-start.10 = (f32[16,16]{1,0:T(8,128)S(1)}, f32[16,16]{1,0:T(8,128)S(1)}, u32[]{:S(2)}, u32[]{:S(2)}) collective-permute-start(f32[16,16]{1,0:T(8,128)S(1)} %add.18), channel_id=1, source_target_pairs={{0,24},{4,28},{8,16},{12,20},{16,8},{20,12},{24,0},{28,4},{1,25},{... | collective-permute-start | bytes 3080 | tf_op jit(solution)/shard_map/ppermute | solution.py:384
  59.1 4.6 %collective-permute-start.9 = (f32[16,16]{1,0:T(8,128)S(1)}, f32[16,16]{1,0:T(8,128)S(1)}, u32[]{:S(2)}, u32[]{:S(2)}) collective-permute-start(f32[16,16]{1,0:T(8,128)S(1)} %add.18), channel_id=1, source_target_pairs={{0,16},{4,20},{8,24},{12,28},{16,0},{20,4},{24,8},{28,12},{1,17},{... | collective-permute-start | bytes 3080 | tf_op jit(solution)/shard_map/ppermute | solution.py:384
  59.1 4.6 %collective-permute-start.8 = (f32[16,16]{1,0:T(8,128)S(1)}, f32[16,16]{1,0:T(8,128)S(1)}, u32[]{:S(2)}, u32[]{:S(2)}) collective-permute-start(f32[16,16]{1,0:T(8,128)S(1)} %add.18), channel_id=1, source_target_pairs={{0,8},{4,12},{8,0},{12,4},{16,24},{20,28},{24,16},{28,20},{1,9},{5... | collective-permute-start | bytes 3080 | tf_op jit(solution)/shard_map/ppermute | solution.py:384
  63.7 1.2 %collective-permute-start.11 = (f32[16,16]{1,0:T(8,128)S(1)}, f32[16,16]{1,0:T(8,128)S(1)}, u32[]{:S(2)}, u32[]{:S(2)}) collective-permute-start(f32[16,16]{1,0:T(8,128)S(1)} %add_add_fusion), channel_id=1, source_target_pairs={{0,1},{1,0},{2,3},{3,2},{4,5},{5,4},{6,7},{7,6},{8,9},{9,8},{10,11... | collective-permute-start | bytes 3080 | tf_op jit(solution)/shard_map/ppermute | solution.py:390
  64.9 3.7 %collective-permute-start.12 = (f32[16,16]{1,0:T(8,128)S(1)}, f32[16,16]{1,0:T(8,128)S(1)}, u32[]{:S(2)}, u32[]{:S(2)}) collective-permute-start(f32[16,16]{1,0:T(8,128)S(1)} %add.22), channel_id=1, source_target_pairs={{0,2},{1,3},{2,0},{3,1},{4,6},{5,7},{6,4},{7,5},{8,10},{9,11},{10,... | collective-permute-start | bytes 3080 | tf_op jit(solution)/shard_map/ppermute | solution.py:390
  66.2 4.2 %collective-permute-start.14 = (f32[16,10,8,128]{3,2,1,0:T(8,128)S(1)}, f32[16,10,8,128]{3,2,1,0:T(8,128)S(1)}, u32[]{:S(2)}, u32[]{:S(2)}) collective-permute-start(f32[16,10,8,128]{3,2,1,0:T(8,128)S(1)} %all_to_all.5.y_ref.refs_0_), channel_id=1, source_target_pairs={{0,1},{1,0},{2,3},{3,2},{4,5},{5,4},{6,7},{7,6},{8,9},{9,8},{10,11... | collective-permute-start | bytes 1966088 | tf_op jit(solution)/shard_map/ppermute | solution.py:378
  68.6 2.1 %collective-permute-start.15 = (f32[16,10,8,128]{3,2,1,0:T(8,128)S(1)}, f32[16,10,8,128]{3,2,1,0:T(8,128)S(1)}, u32[]{:S(2)}, u32[]{:S(2)}) collective-permute-start(f32[16,10,8,128]{3,2,1,0:T(8,128)S(1)} %collective-permute-done.13.refs_2_), channel_id=1, source_target_pairs={{0,1},{1,0},{2,3},{3,2},{4,5},{5,4},{6,7},{7,6},{8,9},{9,8},{10,11... | collective-permute-start | bytes 1966088 | tf_op jit(solution)/shard_map/ppermute | solution.py:392

commit v4 on v3

--- a/solution.py
+++ b/solution.py
@@ -250,23 +250,43 @@
     count, comp = y_ref.shape[:2]
     rows = count * SUB
     pair = (((1,), (1,)), ((), ()))
-    total = jnp.zeros((rows, rows), jnp.float32)
-    for c in range(comp):
-        part = y_ref[:, c].reshape(rows, LANE)
-        total = total + lax.dot_general(part, part, pair, precision=EXACT, preferred_element_type=jnp.float32)
+
+    def times(a, b):
+        return lax.dot_general(a, b, pair, preferred_element_type=jnp.float32)
+
+    even = jnp.zeros((rows, rows), jnp.float32)
+    mixed = jnp.zeros((rows, rows), jnp.float32)
+    for c in range(0, comp, 2):
+        x = jnp.concatenate([y_ref[:, c].reshape(rows, LANE), y_ref[:, c + 1].reshape(rows, LANE)], axis=1)
+        high = x.astype(jnp.bfloat16)
+        rest = x - high.astype(jnp.float32)
+        mid = rest.astype(jnp.bfloat16)
+        low = (rest - mid.astype(jnp.float32)).astype(jnp.bfloat16)
+        even = even + times(high, high) + times(mid, mid)
+        mixed = mixed + times(high, mid) + times(high, low)
     row = lax.broadcasted_iota(jnp.int32, (rows, rows), 0)
     col = lax.broadcasted_iota(jnp.int32, (rows, rows), 1)
-    total = jnp.where(lax.rem(row, SUB) == lax.rem(col, SUB), total, 0.0)
+    same = lax.rem(row, SUB) == lax.rem(col, SUB)
+
+    def gather(total):
+        return jnp.sum(jnp.where(same, total, 0.0).reshape(count, SUB, rows), axis=1)
+
     owner = lax.div(lax.broadcasted_iota(jnp.int32, (count, rows), 1), SUB)
     member = (owner == lax.broadcasted_iota(jnp.int32, (count, rows), 0)).astype(jnp.float32)
-    half = lax.dot_general(member, total, (((1,), (0,)), ((), ())), precision=EXACT, preferred_element_type=jnp.float32)
-    g_ref[...] = lax.dot_general(half, member, pair, precision=EXACT, preferred_element_type=jnp.float32)
-
-
-def gram(y):
+    one = gather(mixed)
+    both = gather(even) + one
+    exact = functools.partial(lax.dot_general, precision=EXACT, preferred_element_type=jnp.float32)
+    g = exact(both, member, pair) + exact(member, one, pair)
+    g = jnp.concatenate([g, jnp.zeros((count, LANE - count), jnp.float32)], axis=1)
+    for x in range(g_ref.shape[0]):
+        g_ref[x] = g
+
+
+def gram(y, copies):
+    count = y.shape[0]
     return pl.pallas_call(
         gram_kernel,
-        out_shape=jax.ShapeDtypeStruct((y.shape[0],) * 2, jnp.float32),
+        out_shape=jax.ShapeDtypeStruct((copies, count, LANE), jnp.float32),
         in_specs=[pl.BlockSpec(memory_space=pltpu.VMEM)],
         out_specs=pl.BlockSpec(memory_space=pltpu.VMEM),
         compiler_params=pltpu.CompilerParams(vmem_limit_bytes=4 << 20),
@@ -275,11 +295,30 @@
     )(y)
 
 
-def factor_kernel(length, g_ref, coeff_ref, linv_ref):
-    n = g_ref.shape[0]
+def add_kernel(parts_ref, out_ref):
+    total = parts_ref[0]
+    for x in range(1, parts_ref.shape[0]):
+        total = total + parts_ref[x]
+    out_ref[...] = total
+
+
+def add_up(parts):
+    return pl.pallas_call(
+        add_kernel,
+        out_shape=jax.ShapeDtypeStruct(parts.shape[1:], jnp.float32),
+        in_specs=[pl.BlockSpec(memory_space=pltpu.VMEM)],
+        out_specs=pl.BlockSpec(memory_space=pltpu.VMEM),
+        compiler_params=pltpu.CompilerParams(vmem_limit_bytes=2 << 20),
+        name="add",
+    )(parts)
+
+
+def factor_kernel(length, near_ref, far_ref, coeff_ref, linv_ref):
+    n = coeff_ref.shape[0]
     row = lax.broadcasted_iota(jnp.int32, (n, n), 0)
     col = lax.broadcasted_iota(jnp.int32, (n, n), 1)
-    left, right = g_ref[...], (row == col).astype(jnp.float32)
+    left = (near_ref[...] + far_ref[...])[:, :n]
+    right = (row == col).astype(jnp.float32)
     upper, lower = jnp.zeros((n, n), jnp.float32), jnp.zeros((n, n), jnp.float32)
     for k in range(n):
         pivot = left[k : k + 1, k : k + 1]
@@ -294,16 +333,16 @@
     linv_ref[...] = lower * jnp.sqrt(jnp.float32(length))
 
 
-def factor(g, length):
-    square = jax.ShapeDtypeStruct(g.shape, jnp.float32)
+def factor(near, far, length):
+    square = jax.ShapeDtypeStruct((near.shape[0],) * 2, jnp.float32)
     return pl.pallas_call(
         functools.partial(factor_kernel, length),
         out_shape=(square, square),
-        in_specs=[pl.BlockSpec(memory_space=pltpu.VMEM)],
+        in_specs=[pl.BlockSpec(memory_space=pltpu.VMEM)] * 2,
         out_specs=(pl.BlockSpec(memory_space=pltpu.VMEM),) * 2,
         compiler_params=pltpu.CompilerParams(vmem_limit_bytes=1 << 20),
         name="factor",
-    )(g)
+    )(near, far)
 
 
 def basis_kernel(linv_ref, *refs):
@@ -376,22 +415,13 @@
     ys = [y] + [None] * (size_f - 1)
     ys[2] = lax.ppermute(y, "af", [(a, a ^ 2) for a in range(size_f)])
     ys[1] = lax.ppermute(y, "af", [(a, a ^ 1) for a in range(size_f)])
-    g = gram(y)
-    step = 1
-    while step < size_x:
-        far = min(4, size_x // step) if step > 1 else 2
-        others = [
-            lax.ppermute(g, "gx", [(x, x ^ (step * k)) for x in range(size_x)]) for k in range(1, far)
-        ]
-        for other in others:
-            g = g + other
-        step *= far
-    for k in (1, 2):
-        g = g + lax.ppermute(g, "af", [(x, x ^ k) for x in range(size_f)])
-    g, ys[2] = lax.optimization_barrier((g, ys[2]))
+    g = add_up(lax.all_to_all(gram(y, size_x), "gx", 0, 0, tiled=True))
+    g = g + lax.ppermute(g, "af", [(x, x ^ 1) for x in range(size_f)])
+    far = lax.ppermute(g, "af", [(x, x ^ 2) for x in range(size_f)])
+    far, ys[2] = lax.optimization_barrier((far, ys[2]))
     ys[3] = lax.ppermute(ys[2], "af", [(x, x ^ 1) for x in range(size_f)])
     length = parts * planes * nvar * rad * azi * size_x
-    coeff, linv = factor(g, length)
+    coeff, linv = factor(g, far, length)
     return basis_of(linv, ys, forcing.shape), coeff
 
 

time: 72.7 us -> 71.3 us (0.981)
  blocking collectives: 14.5 us -> 26 us
  waiting for transfers between devices: 21.7 us -> 15 us
  starting transfers between devices: 15.6 us -> 10.6 us
  Pallas kernels: 19.8 us -> 18.7 us
    all_to_all x0 -> x1, blocking collectives: none -> 11.5 us  [on_device(): g = add_up(lax.all_to_all(gram(y, size_x), 'gx', 0, 0, tiled=True))]
    ppermute x6 -> x2, waiting for transfers between devices: 10.2 us -> 3.52 us  [the longest x1 2.37 us: on_device(): far = lax.ppermute(g, 'af', [(x, x ^ 2) for x in range(size_f)])]
    ppermute x6 -> x2, starting transfers between devices: 6.33 us -> 1.35 us  [the longest x1 1.28 us: on_device(): far = lax.ppermute(g, 'af', [(x, x ^ 2) for x in range(size_f)])]
    pallas_call x1 -> x2, Pallas kernels: 1.85 us -> 0.7 us  [the longest x1 0.69 us: gram(): pl.pallas_call(gram_kernel, out_shape=jax.ShapeDtypeStruct((copies, count...]
  transfers between devices with their start and end apart: 16 -> 12, of which waited for: 10 -> 7; matrix products, arithmetic and copies ran while one was open for 0% -> 0% of each run, Pallas kernels for 16% -> 14%
where the time goes in v4:
time: 71.3 us; the launch traced here: 71 us
  blocking collectives  26 us (36%)
  Pallas kernels  18.7 us (26%)
  waiting for transfers between devices  15 us (21%)
  starting transfers between devices  10.6 us (15%)
    all_to_all x1, blocking collectives, on_device(): lax.all_to_all(z, ('gx', 'af'), 0, 0, axis_index_groups=together, tiled=T...  14.5 us
    pallas_call x2, Pallas kernels, sweeps(): pl.pallas_call(functools.partial(sweep_kernel, dims, two_sided, bool(stat...  13.2 us
    all_to_all x1, blocking collectives, on_device(): g = add_up(lax.all_to_all(gram(y, size_x), 'gx', 0, 0, tiled=True))  11.5 us
    ppermute x3, waiting for transfers between devices, on_device(): mine.append(lax.ppermute(slabs[k], 'gx', pairs))  9.08 us
    ppermute x3, starting transfers between devices, on_device(): mine.append(lax.ppermute(slabs[k], 'gx', pairs))  4.61 us
    ppermute x4, starting transfers between devices, on_device(): halo.append(lax.ppermute(slabs[k], 'gx', pairs))  3.9 us
    ppermute x1, waiting for transfers between devices, on_device(): far = lax.ppermute(g, 'af', [(x, x ^ 2) for x in range(size_f)])  2.37 us
    ppermute x4, waiting for transfers between devices, on_device(): halo.append(lax.ppermute(slabs[k], 'gx', pairs))  2.14 us
  transfers between devices with their start and end apart: 12, of which 7 were waited for; matrix products, arithmetic and copies ran while one was open for 0% of the time, Pallas kernels for 14%

profile of v4, /device:TPU:0, one launch (start us, length us, event | category | flops | bytes accessed | tf_op | source)
XLA Modules:
  0.0 71.0 jit_solution(5551610946208867727)
XLA Ops:
  0.6 1.2 %pack.1 = (f32[48,8,128]{2,1,0:T(8,128)S(1)}, f32[48,8,128]{2,1,0:T(8,128)S(1)}, f32[48,8,128]{2,1,0:T(8,128)S(1)}, f32[48,8,128]{2,1,0:T(8,128)S(1)}) custom-call(f32[4,2,4,5,4,256]{5,4,3,2,1,0:T(4,128)} %forcing_hbm.1, f32[4,4,256]{2,1,0:T(4,128)} %sponge_hbm.1, f32[4,4,256]{2,1,0:T(4,128)} %flow_hbm.1), custom_call_target="tpu_custom_call" | custom-call | tf_op jit(solution)/shard_map/pack/pallas_call | solution.py:60
  1.9 3.0 %collective-permute-start.4 = (f32[48,8,128]{2,1,0:T(8,128)S(1)}, f32[48,8,128]{2,1,0:T(8,128)S(1)}, u32[]{:S(2)}, u32[]{:S(2)}) collective-permute-start(f32[48,8,128]{2,1,0:T(8,128)S(1)} %get-tuple-element.20), channel_id=1, source_target_pairs={{0,4},{4,0},{8,12},{12,8},{16,20},{20,16},{24,28},{28,24},{1,5},{5... | collective-permute-start | bytes 589832 | tf_op jit(solution)/shard_map/ppermute | solution.py:407
  4.9 1.6 %collective-permute-start.5 = (f32[48,8,128]{2,1,0:T(8,128)S(1)}, f32[48,8,128]{2,1,0:T(8,128)S(1)}, u32[]{:S(2)}, u32[]{:S(2)}) collective-permute-start(f32[48,8,128]{2,1,0:T(8,128)S(1)} %get-tuple-element.21), channel_id=1, source_target_pairs={{0,8},{4,12},{8,0},{12,4},{16,24},{20,28},{24,16},{28,20},{1,9},{5... | collective-permute-start | bytes 589832 | tf_op jit(solution)/shard_map/ppermute | solution.py:407
  6.5 1.3 %collective-permute-start.1 = (f32[48,8,128]{2,1,0:T(8,128)S(1)}, f32[48,8,128]{2,1,0:T(8,128)S(1)}, u32[]{:S(2)}, u32[]{:S(2)}) collective-permute-start(f32[48,8,128]{2,1,0:T(8,128)S(1)} %get-tuple-element.20), channel_id=1, source_target_pairs={{8,28},{12,24},{16,4},{20,0},{9,29},{13,25},{17,5},{21,1},{10,30},... | collective-permute-start | bytes 589832 | tf_op jit(solution)/shard_map/ppermute | solution.py:403
  7.8 0.7 collective-permute-start.2
  8.4 1.4 %collective-permute-done.4.refs_3_ = f32[48,8,128]{2,1,0:T(8,128)S(1)} collective-permute-done((f32[48,8,128]{2,1,0:T(8,128)S(1)}, f32[48,8,128]{2,1,0:T(8,128)S(1)}, u32[]{:S(2)}, u32[]{:S(2)}) %collective-permute-start.4) | collective-permute-done | bytes 196640 | tf_op jit(solution)/shard_map/ppermute | solution.py:407
  9.8 0.7 collective-permute-start.3
  10.5 6.4 %collective-permute-done.5.refs_4_ = f32[48,8,128]{2,1,0:T(8,128)S(1)} collective-permute-done((f32[48,8,128]{2,1,0:T(8,128)S(1)}, f32[48,8,128]{2,1,0:T(8,128)S(1)}, u32[]{:S(2)}, u32[]{:S(2)}) %collective-permute-start.5) | collective-permute-done | bytes 196640 | tf_op jit(solution)/shard_map/ppermute | solution.py:407
  16.9 1.3 %collective-permute-start = (f32[48,8,128]{2,1,0:T(8,128)S(1)}, f32[48,8,128]{2,1,0:T(8,128)S(1)}, u32[]{:S(2)}, u32[]{:S(2)}) collective-permute-start(f32[48,8,128]{2,1,0:T(8,128)S(1)} %get-tuple-element.19.refs_2_), channel_id=1, source_target_pairs={{8,24},{12,28},{16,0},{20,4},{9,25},{13,29},{17,1},{21,5},{10,26},... | collective-permute-start | bytes 589832 | tf_op jit(solution)/shard_map/ppermute | solution.py:403
  18.2 1.3 %collective-permute-done.6.refs_5_ = f32[48,8,128]{2,1,0:T(8,128)S(1)} collective-permute-done((f32[48,8,128]{2,1,0:T(8,128)S(1)}, f32[48,8,128]{2,1,0:T(8,128)S(1)}, u32[]{:S(2)}, u32[]{:S(2)}) %collective-permute-start.6) | collective-permute-done | bytes 196640 | tf_op jit(solution)/shard_map/ppermute | solution.py:407
  19.5 7.6 %inner.1 = (f32[16,10,8,128]{3,2,1,0:T(8,128)S(1)}, f32[260,8,128]{2,1,0:T(8,128)S(1)}, f32[260,8,128]{2,1,0:T(8,128)S(1)}, f32[260,8,128]{2,1,0:T(8,128)S(1)}, ...) custom-call(f32[5,5]{1,0:T(8,128)} %refs_0_.3, ...), custom_call_target="tpu_custom_call" | custom-call | flops 6000000000 | bytes 1048576 | tf_op jit(solution)/shard_map/inner/pallas_call | solution.py:229
  27.1 2.1 %collective-permute-done.refs_2_ = f32[48,8,128]{2,1,0:T(8,128)S(1)} collective-permute-done((f32[48,8,128]{2,1,0:T(8,128)S(1)}, f32[48,8,128]{2,1,0:T(8,128)S(1)}, u32[]{:S(2)}, u32[]{:S(2)}) %collective-permute-start) | collective-permute-done | bytes 196640 | tf_op jit(solution)/shard_map/ppermute | solution.py:403
  29.2 5.7 %outer.1 = (f32[16,10,8,128]{3,2,1,0:T(8,128)S(1)}, f32[260,8,128]{2,1,0:T(8,128)S(1)}, f32[260,8,128]{2,1,0:T(8,128)S(1)}, f32[260,8,128]{2,1,0:T(8,128)S(1)}, ...) custom-call(f32[5,5]{1,0:T(8,128)} %refs_0_.3, ...), custom_call_target="tpu_custom_call", output_to_operand_aliasing={{0}: (6, {}), {1}: (7, {}), {2}: (8, {}), {3}: (9, {}), {4}... | custom-call | flops 6000000000 | bytes 1048576 | tf_op jit(solution)/shard_map/outer/pallas_call | solution.py:229
  34.9 14.5 %all_to_all.10.y_ref.refs_0_ = f32[16,10,8,128]{3,2,1,0:T(8,128)S(1)} all-to-all(f32[16,10,8,128]{3,2,1,0:T(8,128)S(1)} %get-tuple-element.31), channel_id=1, replica_groups={{0,4,8,12,1,5,9,13,2,6,10,14,3,7,11,15},{16,20,24,28,17,21,25,29,18,22,..., dimensions={0} | all-to-all | bytes 1310720 | tf_op jit(solution)/shard_map/all_to_all | solution.py:414
  49.4 0.7 %collective-permute-start.9 = (f32[16,10,8,128]{3,2,1,0:T(8,128)S(1)}, f32[16,10,8,128]{3,2,1,0:T(8,128)S(1)}, u32[]{:S(2)}, u32[]{:S(2)}) collective-permute-start(f32[16,10,8,128]{3,2,1,0:T(8,128)S(1)} %all_to_all.10.y_ref.refs_0_), channel_id=1, source_target_pairs={{0,2},{1,3},{2,0},{3,1},{4,6},{5,7},{6,4},{7,5},{8,10},{9,11},{10,... | collective-permute-start | bytes 1966088 | tf_op jit(solution)/shard_map/ppermute | solution.py:416
  50.1 0.7 gram.1
  50.8 11.5 %all_to_all.11.parts_ref = f32[8,16,128]{2,1,0:T(8,128)S(1)} all-to-all(f32[8,16,128]{2,1,0:T(8,128)S(1)} %gram.1), channel_id=1, replica_groups=mesh['gx'=8,'af'=4] {'gx'}, dimensions={0} | all-to-all | bytes 131072 | tf_op jit(solution)/shard_map/all_to_all | solution.py:418
  62.3 0.1 collective-permute-start.7
  62.4 1.2 %collective-permute-done.7 = f32[16,128]{1,0:T(8,128)S(1)} collective-permute-done((f32[16,128]{1,0:T(8,128)S(1)}, f32[16,128]{1,0:T(8,128)S(1)}, u32[]{:S(2)}, u32[]{:S(2)}) %collective-permute-start.7) | collective-permute-done | bytes 8224 | tf_op jit(solution)/shard_map/ppermute | solution.py:419
  63.5 1.3 %collective-permute-start.8 = (f32[16,128]{1,0:T(8,128)S(1)}, f32[16,128]{1,0:T(8,128)S(1)}, u32[]{:S(2)}, u32[]{:S(2)}) collective-permute-start(f32[16,128]{1,0:T(8,128)S(1)} %add.4.near_ref), channel_id=1, source_target_pairs={{0,2},{1,3},{2,0},{3,1},{4,6},{5,7},{6,4},{7,5},{8,10},{9,11},{10,... | collective-permute-start | bytes 24584 | tf_op jit(solution)/shard_map/ppermute | solution.py:420
  64.8 2.4 %collective-permute-done.8.far_ref = f32[16,128]{1,0:T(8,128)S(1)} collective-permute-done((f32[16,128]{1,0:T(8,128)S(1)}, f32[16,128]{1,0:T(8,128)S(1)}, u32[]{:S(2)}, u32[]{:S(2)}) %collective-permute-start.8) | collective-permute-done | bytes 8224 | tf_op jit(solution)/shard_map/ppermute | solution.py:420
  67.2 1.9 %factor.1 = (f32[16,16]{1,0:T(8,128)}, f32[16,16]{1,0:T(8,128)S(1)}) custom-call(f32[16,128]{1,0:T(8,128)S(1)} %add.4.near_ref, f32[16,128]{1,0:T(8,128)S(1)} %collective-permute-done.8.far_ref), custom_call_target="tpu_custom_call" | custom-call | tf_op jit(solution)/shard_map/factor/pallas_call | solution.py:338
  69.1 0.2 collective-permute-done.11.refs_3_
  69.3 1.7 %basis.1 = f32[4,2,4,5,4,256]{5,4,3,2,1,0:T(4,128)} custom-call(f32[16,16]{1,0:T(8,128)S(1)} %get-tuple-element.33.linv_ref, f32[16,10,8,128]{3,2,1,0:T(8,128)S(1)} %all_to_all.10.y_ref.refs_0_, f32[16,10,8,128]{3,2,1,0:T(8,128)S(1)} %collective-permute-done.10.refs_1_, f32[16,10,8,128]{3,2,1,0:T(8,128)S(1)} %collective-permute-done.9.refs_2_, ...), custom_call_target="tpu_custom_call" | custom-call | tf_op jit(solution)/shard_map/basis/pallas_call | solution.py:375
  (10 shorter events, 0.0 us)
Async XLA Ops:
  1.9 7.9 %collective-permute-start.4 = (f32[48,8,128]{2,1,0:T(8,128)S(1)}, f32[48,8,128]{2,1,0:T(8,128)S(1)}, u32[]{:S(2)}, u32[]{:S(2)}) collective-permute-start(f32[48,8,128]{2,1,0:T(8,128)S(1)} %get-tuple-element.20), channel_id=1, source_target_pairs={{0,4},{4,0},{8,12},{12,8},{16,20},{20,16},{24,28},{28,24},{1,5},{5... | collective-permute-start | bytes 589832 | tf_op jit(solution)/shard_map/ppermute | solution.py:407
  4.9 12.0 %collective-permute-start.5 = (f32[48,8,128]{2,1,0:T(8,128)S(1)}, f32[48,8,128]{2,1,0:T(8,128)S(1)}, u32[]{:S(2)}, u32[]{:S(2)}) collective-permute-start(f32[48,8,128]{2,1,0:T(8,128)S(1)} %get-tuple-element.21), channel_id=1, source_target_pairs={{0,8},{4,12},{8,0},{12,4},{16,24},{20,28},{24,16},{28,20},{1,9},{5... | collective-permute-start | bytes 589832 | tf_op jit(solution)/shard_map/ppermute | solution.py:407
  6.5 13.0 %collective-permute-start.6 = (f32[48,8,128]{2,1,0:T(8,128)S(1)}, f32[48,8,128]{2,1,0:T(8,128)S(1)}, u32[]{:S(2)}, u32[]{:S(2)}) collective-permute-start(f32[48,8,128]{2,1,0:T(8,128)S(1)} %get-tuple-element.22), channel_id=1, source_target_pairs={{0,12},{4,8},{8,4},{12,0},{16,28},{20,24},{24,20},{28,16},{1,13},{... | collective-permute-start | bytes 589832 | tf_op jit(solution)/shard_map/ppermute | solution.py:407
  6.5 22.7 %collective-permute-start.1 = (f32[48,8,128]{2,1,0:T(8,128)S(1)}, f32[48,8,128]{2,1,0:T(8,128)S(1)}, u32[]{:S(2)}, u32[]{:S(2)}) collective-permute-start(f32[48,8,128]{2,1,0:T(8,128)S(1)} %get-tuple-element.20), channel_id=1, source_target_pairs={{8,28},{12,24},{16,4},{20,0},{9,29},{13,25},{17,5},{21,1},{10,30},... | collective-permute-start | bytes 589832 | tf_op jit(solution)/shard_map/ppermute | solution.py:403
  7.8 21.4 %collective-permute-start.2 = (f32[48,8,128]{2,1,0:T(8,128)S(1)}, f32[48,8,128]{2,1,0:T(8,128)S(1)}, u32[]{:S(2)}, u32[]{:S(2)}) collective-permute-start(f32[48,8,128]{2,1,0:T(8,128)S(1)} %get-tuple-element.21), channel_id=1, source_target_pairs={{8,16},{12,20},{16,8},{20,12},{9,17},{13,21},{17,9},{21,13},{10,18... | collective-permute-start | bytes 589832 | tf_op jit(solution)/shard_map/ppermute | solution.py:403
  9.8 19.4 %collective-permute-start.3 = (f32[48,8,128]{2,1,0:T(8,128)S(1)}, f32[48,8,128]{2,1,0:T(8,128)S(1)}, u32[]{:S(2)}, u32[]{:S(2)}) collective-permute-start(f32[48,8,128]{2,1,0:T(8,128)S(1)} %get-tuple-element.22), channel_id=1, source_target_pairs={{8,20},{12,16},{16,12},{20,8},{9,21},{13,17},{17,13},{21,9},{10,22... | collective-permute-start | bytes 589832 | tf_op jit(solution)/shard_map/ppermute | solution.py:403
  16.9 12.3 %collective-permute-start = (f32[48,8,128]{2,1,0:T(8,128)S(1)}, f32[48,8,128]{2,1,0:T(8,128)S(1)}, u32[]{:S(2)}, u32[]{:S(2)}) collective-permute-start(f32[48,8,128]{2,1,0:T(8,128)S(1)} %get-tuple-element.19.refs_2_), channel_id=1, source_target_pairs={{8,24},{12,28},{16,0},{20,4},{9,25},{13,29},{17,1},{21,5},{10,26},... | collective-permute-start | bytes 589832 | tf_op jit(solution)/shard_map/ppermute | solution.py:403
  49.4 17.8 %collective-permute-start.9 = (f32[16,10,8,128]{3,2,1,0:T(8,128)S(1)}, f32[16,10,8,128]{3,2,1,0:T(8,128)S(1)}, u32[]{:S(2)}, u32[]{:S(2)}) collective-permute-start(f32[16,10,8,128]{3,2,1,0:T(8,128)S(1)} %all_to_all.10.y_ref.refs_0_), channel_id=1, source_target_pairs={{0,2},{1,3},{2,0},{3,1},{4,6},{5,7},{6,4},{7,5},{8,10},{9,11},{10,... | collective-permute-start | bytes 1966088 | tf_op jit(solution)/shard_map/ppermute | solution.py:416
  62.3 1.2 %collective-permute-start.7 = (f32[16,128]{1,0:T(8,128)S(1)}, f32[16,128]{1,0:T(8,128)S(1)}, u32[]{:S(2)}, u32[]{:S(2)}) collective-permute-start(f32[16,128]{1,0:T(8,128)S(1)} %add.5), channel_id=1, source_target_pairs={{0,1},{1,0},{2,3},{3,2},{4,5},{5,4},{6,7},{7,6},{8,9},{9,8},{10,11... | collective-permute-start | bytes 24584 | tf_op jit(solution)/shard_map/ppermute | solution.py:419
  63.5 3.7 %collective-permute-start.8 = (f32[16,128]{1,0:T(8,128)S(1)}, f32[16,128]{1,0:T(8,128)S(1)}, u32[]{:S(2)}, u32[]{:S(2)}) collective-permute-start(f32[16,128]{1,0:T(8,128)S(1)} %add.4.near_ref), channel_id=1, source_target_pairs={{0,2},{1,3},{2,0},{3,1},{4,6},{5,7},{6,4},{7,5},{8,10},{9,11},{10,... | collective-permute-start | bytes 24584 | tf_op jit(solution)/shard_map/ppermute | solution.py:420
  64.8 4.2 %collective-permute-start.10 = (f32[16,10,8,128]{3,2,1,0:T(8,128)S(1)}, f32[16,10,8,128]{3,2,1,0:T(8,128)S(1)}, u32[]{:S(2)}, u32[]{:S(2)}) collective-permute-start(f32[16,10,8,128]{3,2,1,0:T(8,128)S(1)} %all_to_all.10.y_ref.refs_0_), channel_id=1, source_target_pairs={{0,1},{1,0},{2,3},{3,2},{4,5},{5,4},{6,7},{7,6},{8,9},{9,8},{10,11... | collective-permute-start | bytes 1966088 | tf_op jit(solution)/shard_map/ppermute | solution.py:417
  67.2 2.1 %collective-permute-start.11 = (f32[16,10,8,128]{3,2,1,0:T(8,128)S(1)}, f32[16,10,8,128]{3,2,1,0:T(8,128)S(1)}, u32[]{:S(2)}, u32[]{:S(2)}) collective-permute-start(f32[16,10,8,128]{3,2,1,0:T(8,128)S(1)} %collective-permute-done.9.refs_2_), channel_id=1, source_target_pairs={{0,1},{1,0},{2,3},{3,2},{4,5},{5,4},{6,7},{7,6},{8,9},{9,8},{10,11... | collective-permute-start | bytes 1966088 | tf_op jit(solution)/shard_map/ppermute | solution.py:422

commit v5 on v4

--- a/solution.py
+++ b/solution.py
@@ -162,27 +162,28 @@
     def update(i, src, emit):
         field = [src[(i + 1) * comp + c] for c in range(comp)]
         lo, hi = w_lo[i], w_hi[i]
+        lines = src.reshape(src.shape[0] * SUB, LANE)
+        start = (i + 1) * comp * SUB
         for v in range(nvar):
             sums = []
             for part in range(parts):
                 c = part * nvar + v
                 z = field[c]
                 other = pltpu.roll(z, SUB // 2, 0)
-                total = pltpu.roll(jnp.where(at_last, other, z), 1, 1)
-                total = total + pltpu.roll(jnp.where(at_first, other, z), LANE - 1, 1)
-                total = total + jnp.where(at_axis, 0.0, pltpu.roll(z, 1, 0))
-                total = total + jnp.where(at_outer, 0.0, pltpu.roll(z, SUB - 1, 0))
-                total = total + lo * src[i * comp + c]
-                total = total + hi * src[(i + 2) * comp + c]
+                left = pltpu.roll(jnp.where(at_last, other, z), 1, 1)
+                right = pltpu.roll(jnp.where(at_first, other, z), LANE - 1, 1)
+                down = jnp.where(at_axis, 0.0, lines[pl.ds(start + c * SUB - 1, SUB), :])
+                up = jnp.where(at_outer, 0.0, lines[pl.ds(start + c * SUB + 1, SUB), :])
+                total = (lo * src[i * comp + c] + hi * src[(i + 2) * comp + c]) + (down + up)
                 for u in range(nvar):
                     if u != v:
                         total = total + pull[u][v] * field[part * nvar + u]
-                sums.append(total)
+                sums.append(total + (left + right))
             pr, pi = p_re[i * nvar + v], p_im[i * nvar + v]
             emit(i, v, first[(i + 1) * comp + v] + (pr * sums[0] - pi * sums[1]))
             emit(i, nvar + v, first[(i + 1) * comp + nvar + v] + (pr * sums[1] + pi * sums[0]))
 
-    def level(src, emit, lo, hi, unroll=2):
+    def level(src, emit, lo, hi, unroll=8):
         def body(n, _):
             for m in range(unroll):
                 update(lo + n * unroll + m, src, emit)

time: 71.3 us -> 69.3 us (0.972)
  Pallas kernels: 18.7 us -> 13.5 us
  waiting for transfers between devices: 15 us -> 18 us
    pallas_call x2, Pallas kernels: 13.2 us -> 8.08 us  [sweeps(): pl.pallas_call(functools.partial(sweep_kernel, dims, two_sided, bool(stat...]
    ppermute x4, waiting for transfers between devices: 2.14 us -> 5.21 us  [on_device(): halo.append(lax.ppermute(slabs[k], 'gx', pairs))]
  transfers between devices with their start and end apart: 12 -> 12, of which waited for: 7 -> 7; matrix products, arithmetic and copies ran while one was open for 0% -> 0% of each run, Pallas kernels for 14% -> 10%
where the time goes in v5:
time: 69.3 us; the launch traced here: 68.9 us
  blocking collectives  26 us (38%)
  waiting for transfers between devices  18 us (26%)
  Pallas kernels  13.5 us (19%)
  starting transfers between devices  10.6 us (15%)
  between operations  0.71 us (1%)
    all_to_all x1, blocking collectives, on_device(): lax.all_to_all(z, ('gx', 'af'), 0, 0, axis_index_groups=together, tiled=T...  14.5 us
    all_to_all x1, blocking collectives, on_device(): g = add_up(lax.all_to_all(gram(y, size_x), 'gx', 0, 0, tiled=True))  11.5 us
    ppermute x3, waiting for transfers between devices, on_device(): mine.append(lax.ppermute(slabs[k], 'gx', pairs))  9.08 us
    pallas_call x2, Pallas kernels, sweeps(): pl.pallas_call(functools.partial(sweep_kernel, dims, two_sided, bool(stat...  8.08 us
    ppermute x4, waiting for transfers between devices, on_device(): halo.append(lax.ppermute(slabs[k], 'gx', pairs))  5.21 us
    ppermute x3, starting transfers between devices, on_device(): mine.append(lax.ppermute(slabs[k], 'gx', pairs))  4.61 us
    ppermute x4, starting transfers between devices, on_device(): halo.append(lax.ppermute(slabs[k], 'gx', pairs))  3.9 us
    ppermute x1, waiting for transfers between devices, on_device(): far = lax.ppermute(g, 'af', [(x, x ^ 2) for x in range(size_f)])  2.35 us
  transfers between devices with their start and end apart: 12, of which 7 were waited for; matrix products, arithmetic and copies ran while one was open for 0% of the time, Pallas kernels for 10%

profile of v5, /device:TPU:0, one launch (start us, length us, event | category | flops | bytes accessed | tf_op | source)
XLA Modules:
  0.0 68.9 jit_solution(6982118620160452731)
XLA Ops:
  0.6 1.2 %pack.1 = (f32[48,8,128]{2,1,0:T(8,128)S(1)}, f32[48,8,128]{2,1,0:T(8,128)S(1)}, f32[48,8,128]{2,1,0:T(8,128)S(1)}, f32[48,8,128]{2,1,0:T(8,128)S(1)}) custom-call(f32[4,2,4,5,4,256]{5,4,3,2,1,0:T(4,128)} %forcing_hbm.1, f32[4,4,256]{2,1,0:T(4,128)} %sponge_hbm.1, f32[4,4,256]{2,1,0:T(4,128)} %flow_hbm.1), custom_call_target="tpu_custom_call" | custom-call | tf_op jit(solution)/shard_map/pack/pallas_call | solution.py:60
  1.9 3.0 %collective-permute-start.4 = (f32[48,8,128]{2,1,0:T(8,128)S(1)}, f32[48,8,128]{2,1,0:T(8,128)S(1)}, u32[]{:S(2)}, u32[]{:S(2)}) collective-permute-start(f32[48,8,128]{2,1,0:T(8,128)S(1)} %get-tuple-element.20), channel_id=1, source_target_pairs={{0,4},{4,0},{8,12},{12,8},{16,20},{20,16},{24,28},{28,24},{1,5},{5... | collective-permute-start | bytes 589832 | tf_op jit(solution)/shard_map/ppermute | solution.py:408
  4.9 1.6 %collective-permute-start.5 = (f32[48,8,128]{2,1,0:T(8,128)S(1)}, f32[48,8,128]{2,1,0:T(8,128)S(1)}, u32[]{:S(2)}, u32[]{:S(2)}) collective-permute-start(f32[48,8,128]{2,1,0:T(8,128)S(1)} %get-tuple-element.21), channel_id=1, source_target_pairs={{0,8},{4,12},{8,0},{12,4},{16,24},{20,28},{24,16},{28,20},{1,9},{5... | collective-permute-start | bytes 589832 | tf_op jit(solution)/shard_map/ppermute | solution.py:408
  6.5 1.3 %collective-permute-start.1 = (f32[48,8,128]{2,1,0:T(8,128)S(1)}, f32[48,8,128]{2,1,0:T(8,128)S(1)}, u32[]{:S(2)}, u32[]{:S(2)}) collective-permute-start(f32[48,8,128]{2,1,0:T(8,128)S(1)} %get-tuple-element.20), channel_id=1, source_target_pairs={{8,28},{12,24},{16,4},{20,0},{9,29},{13,25},{17,5},{21,1},{10,30},... | collective-permute-start | bytes 589832 | tf_op jit(solution)/shard_map/ppermute | solution.py:404
  7.8 0.7 collective-permute-start.2
  8.4 1.4 %collective-permute-done.4.refs_3_ = f32[48,8,128]{2,1,0:T(8,128)S(1)} collective-permute-done((f32[48,8,128]{2,1,0:T(8,128)S(1)}, f32[48,8,128]{2,1,0:T(8,128)S(1)}, u32[]{:S(2)}, u32[]{:S(2)}) %collective-permute-start.4) | collective-permute-done | bytes 196640 | tf_op jit(solution)/shard_map/ppermute | solution.py:408
  9.8 0.7 collective-permute-start.3
  10.5 6.4 %collective-permute-done.5.refs_4_ = f32[48,8,128]{2,1,0:T(8,128)S(1)} collective-permute-done((f32[48,8,128]{2,1,0:T(8,128)S(1)}, f32[48,8,128]{2,1,0:T(8,128)S(1)}, u32[]{:S(2)}, u32[]{:S(2)}) %collective-permute-start.5) | collective-permute-done | bytes 196640 | tf_op jit(solution)/shard_map/ppermute | solution.py:408
  16.9 1.3 %collective-permute-start = (f32[48,8,128]{2,1,0:T(8,128)S(1)}, f32[48,8,128]{2,1,0:T(8,128)S(1)}, u32[]{:S(2)}, u32[]{:S(2)}) collective-permute-start(f32[48,8,128]{2,1,0:T(8,128)S(1)} %get-tuple-element.19.refs_2_), channel_id=1, source_target_pairs={{8,24},{12,28},{16,0},{20,4},{9,25},{13,29},{17,1},{21,5},{10,26},... | collective-permute-start | bytes 589832 | tf_op jit(solution)/shard_map/ppermute | solution.py:404
  18.2 1.3 %collective-permute-done.6.refs_5_ = f32[48,8,128]{2,1,0:T(8,128)S(1)} collective-permute-done((f32[48,8,128]{2,1,0:T(8,128)S(1)}, f32[48,8,128]{2,1,0:T(8,128)S(1)}, u32[]{:S(2)}, u32[]{:S(2)}) %collective-permute-start.6) | collective-permute-done | bytes 196640 | tf_op jit(solution)/shard_map/ppermute | solution.py:408
  19.5 4.5 %inner.1 = (f32[16,10,8,128]{3,2,1,0:T(8,128)S(1)}, f32[260,8,128]{2,1,0:T(8,128)S(1)}, f32[260,8,128]{2,1,0:T(8,128)S(1)}, f32[260,8,128]{2,1,0:T(8,128)S(1)}, ...) custom-call(f32[5,5]{1,0:T(8,128)} %refs_0_.3, ...), custom_call_target="tpu_custom_call" | custom-call | flops 6000000000 | bytes 1048576 | tf_op jit(solution)/shard_map/inner/pallas_call | solution.py:230
  24.0 5.2 %collective-permute-done.refs_2_ = f32[48,8,128]{2,1,0:T(8,128)S(1)} collective-permute-done((f32[48,8,128]{2,1,0:T(8,128)S(1)}, f32[48,8,128]{2,1,0:T(8,128)S(1)}, u32[]{:S(2)}, u32[]{:S(2)}) %collective-permute-start) | collective-permute-done | bytes 196640 | tf_op jit(solution)/shard_map/ppermute | solution.py:404
  29.2 3.6 %outer.1 = (f32[16,10,8,128]{3,2,1,0:T(8,128)S(1)}, f32[260,8,128]{2,1,0:T(8,128)S(1)}, f32[260,8,128]{2,1,0:T(8,128)S(1)}, f32[260,8,128]{2,1,0:T(8,128)S(1)}, ...) custom-call(f32[5,5]{1,0:T(8,128)} %refs_0_.3, ...), custom_call_target="tpu_custom_call", output_to_operand_aliasing={{0}: (6, {}), {1}: (7, {}), {2}: (8, {}), {3}: (9, {}), {4}... | custom-call | flops 6000000000 | bytes 1048576 | tf_op jit(solution)/shard_map/outer/pallas_call | solution.py:230
  32.8 14.5 %all_to_all.10.y_ref.refs_0_ = f32[16,10,8,128]{3,2,1,0:T(8,128)S(1)} all-to-all(f32[16,10,8,128]{3,2,1,0:T(8,128)S(1)} %get-tuple-element.31), channel_id=1, replica_groups={{0,4,8,12,1,5,9,13,2,6,10,14,3,7,11,15},{16,20,24,28,17,21,25,29,18,22,..., dimensions={0} | all-to-all | bytes 1310720 | tf_op jit(solution)/shard_map/all_to_all | solution.py:415
  47.3 0.7 %collective-permute-start.9 = (f32[16,10,8,128]{3,2,1,0:T(8,128)S(1)}, f32[16,10,8,128]{3,2,1,0:T(8,128)S(1)}, u32[]{:S(2)}, u32[]{:S(2)}) collective-permute-start(f32[16,10,8,128]{3,2,1,0:T(8,128)S(1)} %all_to_all.10.y_ref.refs_0_), channel_id=1, source_target_pairs={{0,2},{1,3},{2,0},{3,1},{4,6},{5,7},{6,4},{7,5},{8,10},{9,11},{10,... | collective-permute-start | bytes 1966088 | tf_op jit(solution)/shard_map/ppermute | solution.py:417
  48.1 0.7 %gram.1 = f32[8,16,128]{2,1,0:T(8,128)S(1)} custom-call(f32[16,10,8,128]{3,2,1,0:T(8,128)S(1)} %all_to_all.10.y_ref.refs_0_), custom_call_target="tpu_custom_call" | custom-call | flops 2000000000 | bytes 1048576 | tf_op jit(solution)/shard_map/gram/pallas_call | solution.py:288
  48.8 11.5 %all_to_all.11.parts_ref = f32[8,16,128]{2,1,0:T(8,128)S(1)} all-to-all(f32[8,16,128]{2,1,0:T(8,128)S(1)} %gram.1), channel_id=1, replica_groups=mesh['gx'=8,'af'=4] {'gx'}, dimensions={0} | all-to-all | bytes 131072 | tf_op jit(solution)/shard_map/all_to_all | solution.py:419
  60.2 0.1 collective-permute-start.7
  60.3 1.2 %collective-permute-done.7 = f32[16,128]{1,0:T(8,128)S(1)} collective-permute-done((f32[16,128]{1,0:T(8,128)S(1)}, f32[16,128]{1,0:T(8,128)S(1)}, u32[]{:S(2)}, u32[]{:S(2)}) %collective-permute-start.7) | collective-permute-done | bytes 8224 | tf_op jit(solution)/shard_map/ppermute | solution.py:420
  61.5 1.3 %collective-permute-start.8 = (f32[16,128]{1,0:T(8,128)S(1)}, f32[16,128]{1,0:T(8,128)S(1)}, u32[]{:S(2)}, u32[]{:S(2)}) collective-permute-start(f32[16,128]{1,0:T(8,128)S(1)} %add.4.near_ref), channel_id=1, source_target_pairs={{0,2},{1,3},{2,0},{3,1},{4,6},{5,7},{6,4},{7,5},{8,10},{9,11},{10,... | collective-permute-start | bytes 24584 | tf_op jit(solution)/shard_map/ppermute | solution.py:421
  62.8 2.4 %collective-permute-done.8.far_ref = f32[16,128]{1,0:T(8,128)S(1)} collective-permute-done((f32[16,128]{1,0:T(8,128)S(1)}, f32[16,128]{1,0:T(8,128)S(1)}, u32[]{:S(2)}, u32[]{:S(2)}) %collective-permute-start.8) | collective-permute-done | bytes 8224 | tf_op jit(solution)/shard_map/ppermute | solution.py:421
  65.1 1.9 %factor.1 = (f32[16,16]{1,0:T(8,128)}, f32[16,16]{1,0:T(8,128)S(1)}) custom-call(f32[16,128]{1,0:T(8,128)S(1)} %add.4.near_ref, f32[16,128]{1,0:T(8,128)S(1)} %collective-permute-done.8.far_ref), custom_call_target="tpu_custom_call" | custom-call | tf_op jit(solution)/shard_map/factor/pallas_call | solution.py:339
  67.0 0.2 collective-permute-done.11.refs_3_
  67.2 1.7 %basis.1 = f32[4,2,4,5,4,256]{5,4,3,2,1,0:T(4,128)} custom-call(f32[16,16]{1,0:T(8,128)S(1)} %get-tuple-element.33.linv_ref, f32[16,10,8,128]{3,2,1,0:T(8,128)S(1)} %all_to_all.10.y_ref.refs_0_, f32[16,10,8,128]{3,2,1,0:T(8,128)S(1)} %collective-permute-done.10.refs_1_, f32[16,10,8,128]{3,2,1,0:T(8,128)S(1)} %collective-permute-done.9.refs_2_, ...), custom_call_target="tpu_custom_call" | custom-call | tf_op jit(solution)/shard_map/basis/pallas_call | solution.py:376
  (10 shorter events, 0.0 us)
Async XLA Ops:
  1.9 7.9 %collective-permute-start.4 = (f32[48,8,128]{2,1,0:T(8,128)S(1)}, f32[48,8,128]{2,1,0:T(8,128)S(1)}, u32[]{:S(2)}, u32[]{:S(2)}) collective-permute-start(f32[48,8,128]{2,1,0:T(8,128)S(1)} %get-tuple-element.20), channel_id=1, source_target_pairs={{0,4},{4,0},{8,12},{12,8},{16,20},{20,16},{24,28},{28,24},{1,5},{5... | collective-permute-start | bytes 589832 | tf_op jit(solution)/shard_map/ppermute | solution.py:408
  4.9 12.0 %collective-permute-start.5 = (f32[48,8,128]{2,1,0:T(8,128)S(1)}, f32[48,8,128]{2,1,0:T(8,128)S(1)}, u32[]{:S(2)}, u32[]{:S(2)}) collective-permute-start(f32[48,8,128]{2,1,0:T(8,128)S(1)} %get-tuple-element.21), channel_id=1, source_target_pairs={{0,8},{4,12},{8,0},{12,4},{16,24},{20,28},{24,16},{28,20},{1,9},{5... | collective-permute-start | bytes 589832 | tf_op jit(solution)/shard_map/ppermute | solution.py:408
  6.5 13.0 %collective-permute-start.6 = (f32[48,8,128]{2,1,0:T(8,128)S(1)}, f32[48,8,128]{2,1,0:T(8,128)S(1)}, u32[]{:S(2)}, u32[]{:S(2)}) collective-permute-start(f32[48,8,128]{2,1,0:T(8,128)S(1)} %get-tuple-element.22), channel_id=1, source_target_pairs={{0,12},{4,8},{8,4},{12,0},{16,28},{20,24},{24,20},{28,16},{1,13},{... | collective-permute-start | bytes 589832 | tf_op jit(solution)/shard_map/ppermute | solution.py:408
  6.5 22.7 %collective-permute-start.1 = (f32[48,8,128]{2,1,0:T(8,128)S(1)}, f32[48,8,128]{2,1,0:T(8,128)S(1)}, u32[]{:S(2)}, u32[]{:S(2)}) collective-permute-start(f32[48,8,128]{2,1,0:T(8,128)S(1)} %get-tuple-element.20), channel_id=1, source_target_pairs={{8,28},{12,24},{16,4},{20,0},{9,29},{13,25},{17,5},{21,1},{10,30},... | collective-permute-start | bytes 589832 | tf_op jit(solution)/shard_map/ppermute | solution.py:404
  7.8 21.4 %collective-permute-start.2 = (f32[48,8,128]{2,1,0:T(8,128)S(1)}, f32[48,8,128]{2,1,0:T(8,128)S(1)}, u32[]{:S(2)}, u32[]{:S(2)}) collective-permute-start(f32[48,8,128]{2,1,0:T(8,128)S(1)} %get-tuple-element.21), channel_id=1, source_target_pairs={{8,16},{12,20},{16,8},{20,12},{9,17},{13,21},{17,9},{21,13},{10,18... | collective-permute-start | bytes 589832 | tf_op jit(solution)/shard_map/ppermute | solution.py:404
  9.8 19.4 %collective-permute-start.3 = (f32[48,8,128]{2,1,0:T(8,128)S(1)}, f32[48,8,128]{2,1,0:T(8,128)S(1)}, u32[]{:S(2)}, u32[]{:S(2)}) collective-permute-start(f32[48,8,128]{2,1,0:T(8,128)S(1)} %get-tuple-element.22), channel_id=1, source_target_pairs={{8,20},{12,16},{16,12},{20,8},{9,21},{13,17},{17,13},{21,9},{10,22... | collective-permute-start | bytes 589832 | tf_op jit(solution)/shard_map/ppermute | solution.py:404
  16.9 12.3 %collective-permute-start = (f32[48,8,128]{2,1,0:T(8,128)S(1)}, f32[48,8,128]{2,1,0:T(8,128)S(1)}, u32[]{:S(2)}, u32[]{:S(2)}) collective-permute-start(f32[48,8,128]{2,1,0:T(8,128)S(1)} %get-tuple-element.19.refs_2_), channel_id=1, source_target_pairs={{8,24},{12,28},{16,0},{20,4},{9,25},{13,29},{17,1},{21,5},{10,26},... | collective-permute-start | bytes 589832 | tf_op jit(solution)/shard_map/ppermute | solution.py:404
  47.3 17.8 %collective-permute-start.9 = (f32[16,10,8,128]{3,2,1,0:T(8,128)S(1)}, f32[16,10,8,128]{3,2,1,0:T(8,128)S(1)}, u32[]{:S(2)}, u32[]{:S(2)}) collective-permute-start(f32[16,10,8,128]{3,2,1,0:T(8,128)S(1)} %all_to_all.10.y_ref.refs_0_), channel_id=1, source_target_pairs={{0,2},{1,3},{2,0},{3,1},{4,6},{5,7},{6,4},{7,5},{8,10},{9,11},{10,... | collective-permute-start | bytes 1966088 | tf_op jit(solution)/shard_map/ppermute | solution.py:417
  60.2 1.2 %collective-permute-start.7 = (f32[16,128]{1,0:T(8,128)S(1)}, f32[16,128]{1,0:T(8,128)S(1)}, u32[]{:S(2)}, u32[]{:S(2)}) collective-permute-start(f32[16,128]{1,0:T(8,128)S(1)} %add.5), channel_id=1, source_target_pairs={{0,1},{1,0},{2,3},{3,2},{4,5},{5,4},{6,7},{7,6},{8,9},{9,8},{10,11... | collective-permute-start | bytes 24584 | tf_op jit(solution)/shard_map/ppermute | solution.py:420
  61.5 3.7 %collective-permute-start.8 = (f32[16,128]{1,0:T(8,128)S(1)}, f32[16,128]{1,0:T(8,128)S(1)}, u32[]{:S(2)}, u32[]{:S(2)}) collective-permute-start(f32[16,128]{1,0:T(8,128)S(1)} %add.4.near_ref), channel_id=1, source_target_pairs={{0,2},{1,3},{2,0},{3,1},{4,6},{5,7},{6,4},{7,5},{8,10},{9,11},{10,... | collective-permute-start | bytes 24584 | tf_op jit(solution)/shard_map/ppermute | solution.py:421
  62.8 4.2 %collective-permute-start.10 = (f32[16,10,8,128]{3,2,1,0:T(8,128)S(1)}, f32[16,10,8,128]{3,2,1,0:T(8,128)S(1)}, u32[]{:S(2)}, u32[]{:S(2)}) collective-permute-start(f32[16,10,8,128]{3,2,1,0:T(8,128)S(1)} %all_to_all.10.y_ref.refs_0_), channel_id=1, source_target_pairs={{0,1},{1,0},{2,3},{3,2},{4,5},{5,4},{6,7},{7,6},{8,9},{9,8},{10,11... | collective-permute-start | bytes 1966088 | tf_op jit(solution)/shard_map/ppermute | solution.py:418
  65.1 2.1 %collective-permute-start.11 = (f32[16,10,8,128]{3,2,1,0:T(8,128)S(1)}, f32[16,10,8,128]{3,2,1,0:T(8,128)S(1)}, u32[]{:S(2)}, u32[]{:S(2)}) collective-permute-start(f32[16,10,8,128]{3,2,1,0:T(8,128)S(1)} %collective-permute-done.9.refs_2_), channel_id=1, source_target_pairs={{0,1},{1,0},{2,3},{3,2},{4,5},{5,4},{6,7},{7,6},{8,9},{9,8},{10,11... | collective-permute-start | bytes 1966088 | tf_op jit(solution)/shard_map/ppermute | solution.py:423
